TPU v7x, 256 devices: a whole 4x4x8 slice. The times are simulated.
256 devices in a mesh: band: 4 (over z_hi, core), grid: 64 (over y, z_lo, x).
Axes of the slice: x: 4, y: 4, z: 8 (z_hi: 2, z_lo: 4; z = z_hi * 4 + z_lo), core: 2. Of those that a mesh axis runs over, the one named last changes fastest.
Arguments:
- orbitals: bfloat16 [256, 384, 32, 128], P('band', 'grid'), may hold values from -24 to 24, as said below
- potential: float32 [384, 32, 128], P('grid'), may hold values from -1 to 1
Outputs:
- gradient: float32 [256, 384, 32, 128], P('band', 'grid')
- intersection: float32 [256, 256], P('band')
- subspace: float32 [256, 256], P('band')
Inputs may be any that keep to these rules, and one draw needn't show every extreme that they name: `orbitals`: orbital values of order one.
All inputs are finite; a program needn't handle non-finite values.
Results may differ from a plain program's by a relative error of at most 0.0003.
Values may be sent and summed in bfloat16 or wider, within the bound.
A program may use at most 128 MiB of HBM per device.

v0:
```python
import jax
import jax.numpy as jnp
from jax import lax
from jax.sharding import PartitionSpec as P

COEFFS = (-49.0 / 18.0, 3.0 / 2.0, -3.0 / 20.0, 1.0 / 90.0)


def padded_2(cells, sides, width):
    for axis, dim in sides:
        count = lax.axis_size(axis)
        head = lax.slice_in_dim(cells, 0, width, axis=dim)
        tail = lax.slice_in_dim(cells, cells.shape[dim] - width, cells.shape[dim], axis=dim)
        cells = jnp.concatenate(
            [
                lax.ppermute(tail, axis, [(i, (i + 1) % count) for i in range(count)]),
                cells,
                lax.ppermute(head, axis, [((i + 1) % count, i) for i in range(count)]),
            ],
            axis=dim,
        )
    return cells


def apply_hamiltonian(padded, potential):
    stencil_reach = len(COEFFS) - 1
    width_x = padded.shape[1] - 2 * stencil_reach
    planes = padded.shape[2]
    center = padded[:, stencil_reach : stencil_reach + width_x].astype(jnp.float32)
    z_padded = jnp.pad(center, ((0, 0), (0, 0), (stencil_reach, stencil_reach), (0, 0)))
    total = 3.0 * COEFFS[0] * center
    for shift_by in range(1, stencil_reach + 1):
        pair_x = padded[:, stencil_reach + shift_by : stencil_reach + shift_by + width_x].astype(
            jnp.float32
        ) + padded[:, stencil_reach - shift_by : stencil_reach - shift_by + width_x].astype(
            jnp.float32
        )
        pair_z = (
            z_padded[:, :, stencil_reach + shift_by : stencil_reach + shift_by + planes]
            + z_padded[:, :, stencil_reach - shift_by : stencil_reach - shift_by + planes]
        )
        pair_y = jnp.roll(center, shift_by, 3) + jnp.roll(center, -shift_by, 3)
        total = total + COEFFS[shift_by] * (pair_x + pair_z + pair_y)
    return -0.5 * total + potential * center


def row_products(left, right):
    return lax.dot_general(
        left, right, (((1,), (1,)), ((), ())), preferred_element_type=jnp.float32
    )


def body(orbitals, potential):
    shape = orbitals.shape
    orb_dev = shape[0]
    cell_count = shape[1] * lax.axis_size("grid") * shape[2] * shape[3]
    group_count = orb_dev // 16
    stencil_reach = len(COEFFS) - 1
    padded = padded_2(orbitals, (("grid", 1),), stencil_reach)
    groups = padded.reshape((group_count, 16) + padded.shape[1:])
    hpsi = lax.map(lambda group: apply_hamiltonian(group, potential), groups).reshape(shape)
    flat_psi = orbitals.reshape(orb_dev, -1)
    flat_h = hpsi.astype(jnp.bfloat16).reshape(orb_dev, -1)
    panel_rows = lax.all_gather(flat_psi, "band", axis=0, tiled=True)
    s_rows = row_products(flat_psi, panel_rows)
    h_rows = row_products(flat_h, panel_rows)
    s_rows, h_rows = (s_rows, h_rows)
    s_summed, h_summed = lax.psum((s_rows, h_rows), "grid")
    intersection = s_summed / cell_count
    subspace = h_summed / cell_count
    offset_rows = lax.axis_index("band") * orb_dev
    s_diag = jnp.diagonal(lax.dynamic_slice_in_dim(intersection, offset_rows, orb_dev, 1))
    h_diag = jnp.diagonal(lax.dynamic_slice_in_dim(subspace, offset_rows, orb_dev, 1))
    rayleigh = h_diag / (s_diag + 1e-06)
    gradient = (hpsi - rayleigh[:, None, None, None] * orbitals.astype(jnp.float32)) / (
        2.0 + potential
    )
    return (gradient, intersection, subspace)


def solution(mesh):
    in_specs = (P("band", "grid", None, None), P("grid", None, None))
    out_specs = (P("band", "grid", None, None), P("band", None), P("band", None))
    return jax.shard_map(body, mesh=mesh, in_specs=in_specs, out_specs=out_specs, check_vma=False)
```

profile of v0, /device:TPU:2, one launch (start us, length us, event | category | flops | bytes accessed | tf_op | source)
XLA Modules:
  0.0 889.9 jit_solution(4659854884611012534)
XLA Ops:
  7.2 5.6 copy.8
  12.9 1.8 copy-done
  14.7 2.3 fusion.27
  19.2 34.2 %collective-permute-done = bf16[64,3,32,128]{3,2,1,0:T(8,128)(2,1)} collective-permute-done((bf16[64,3,32,128]{3,2,1,0:T(8,128)(2,1)}, bf16[64,3,32,128]{3,2,1,0:T(8,128)(2,1)}, u32[]{:S(2)}, u32[]{:S(2)}) %collective-permute-start) | collective-permute-done | bytes 1572896 | tf_op jit(solution)/shard_map/ppermute | solution.py:16
  54.6 5.0 pad_maximum_fusion
  59.6 59.5 %while.12 = (s32[]{:T(128)}, f32[4,16,6,32,128]{4,3,2,1,0:T(8,128)}, bf16[4,16,12,32,128]{4,3,2,1,0:T(8,128)(2,1)}, f32[6,32,128]{2,1,0:T(8,128)S(1)}, s32[]{:T(128)}) while((s32[]{:T(128)}, f32[4,16,6,32,128]{4,3,2,1,0:T(8,128)}, bf16[4,16,12,32,128]{4,3,2,1,0:T(8,128)(2,1)}, f32[6,32,128]{2,1,0:T(8,128)S(1)}, s32[]{:T(128)}) %tuple.59), condition=%wide.region_1.2_spmd, body=%wide.region_0.1_spmd.sunk | while | flops 14942210 | bytes 44888640 | solution.py:61
  63.9 1.7 fusion.43
  65.6 2.3 fusion.44
  67.9 6.6 fusion.45
  78.8 1.7 fusion.43
  80.5 2.3 fusion.44
  82.8 6.6 fusion.45
  95.4 2.2 fusion.44
  97.6 6.8 fusion.45
  108.6 1.7 fusion.43
  110.4 2.2 fusion.44
  112.6 6.6 fusion.45
  119.2 5.3 convert_element_type.56
  124.5 5.0 convert_element_type.57
  129.5 46.6 %all-gather.2.cloned.1.call-done = bf16[256,24576]{1,0:T(8,128)(2,1)} async-done(((bf16[64,24576]{1,0:T(8,128)(2,1)}), bf16[256,24576]{1,0:T(8,128)(2,1)}) %all-gather.2.cloned.1.call-update) | async-done | bytes 12582928 | tf_op jit(solution)/shard_map/all_gather | solution.py:64
  176.2 9.3 %fusion.20 = f32[64,256]{1,0:T(8,128)} fusion(bf16[256,24576]{1,0:T(8,128)(2,1)} %all-gather.2.cloned.1.call-done, bf16[8,8,192,128]{3,2,1,0:T(8,128)(2,1)S(1)} %bitcast.29), kind=kOutput, calls=%fused_computation.43 | convolution fusion | flops 805306368 | bytes 15794176 | tf_op jit(solution)/shard_map/dot_general | solution.py:48
  185.5 9.1 %fusion.28 = f32[64,256]{1,0:T(8,128)} fusion(bf16[64,24576]{1,0:T(8,128)(2,1)S(1)} %copy-done.2, bf16[256,24576]{1,0:T(8,128)(2,1)} %all-gather.2.cloned.1.call-done), kind=kOutput, calls=%fused_computation.51 | convolution fusion | flops 805306368 | bytes 15794176 | tf_op jit(solution)/shard_map/dot_general | solution.py:48
  194.6 678.5 %all-reduce.4.cloned.1.call-done = (f32[64,256]{1,0:T(8,128)}, f32[64,256]{1,0:T(8,128)}) async-done(((f32[64,256]{1,0:T(8,128)}, f32[64,256]{1,0:T(8,128)}), (f32[64,256]{1,0:T(8,128)}, f32[64,256]{1,0:T(8,128)})) %all-reduce.4.cloned.1.call-update) | async-done | bytes 131088 | tf_op jit(solution)/shard_map/psum | solution.py:68
  875.8 7.2 fusion.19
  (52 shorter events, 24.8 us)
Async XLA Ops:
  7.2 169.0 %all-gather.2.cloned.1.call-start = ((), (), s32[]{:S(2)}) async-start(), calls=%async_computation | async-start | bytes 15728640 | tf_op jit(solution)/shard_map/all_gather | solution.py:64
  12.8 1.9 copy-start
  12.9 860.3 %all-reduce.4.cloned.1.call-start = ((), (), s32[]{:S(2)}) async-start(), calls=%async_computation.1 | async-start | bytes 262144 | tf_op jit(solution)/shard_map/psum | solution.py:68
  17.0 36.5 %collective-permute-start = (bf16[64,3,32,128]{3,2,1,0:T(8,128)(2,1)}, bf16[64,3,32,128]{3,2,1,0:T(8,128)(2,1)}, u32[]{:S(2)}, u32[]{:S(2)}) collective-permute-start(bf16[64,3,32,128]{3,2,1,0:T(8,128)(2,1)} %get-tuple-element.79), channel_id=1, source_target_pairs={{0,1},{1,2},{2,3},{3,4},{4,5},{5,6},{6,7},{7,8},{8,9},{9,10},{10,1... | collective-permute-start | bytes 4718600 | tf_op jit(solution)/shard_map/ppermute | solution.py:16
  18.5 36.2 %collective-permute-start.1 = (bf16[64,3,32,128]{3,2,1,0:T(8,128)(2,1)}, bf16[64,3,32,128]{3,2,1,0:T(8,128)(2,1)}, u32[]{:S(2)}, u32[]{:S(2)}) collective-permute-start(bf16[64,3,32,128]{3,2,1,0:T(8,128)(2,1)} %get-tuple-element.80), channel_id=1, source_target_pairs={{1,0},{2,1},{3,2},{4,3},{5,4},{6,5},{7,6},{8,7},{9,8},{10,9},{11,1... | collective-permute-start | bytes 4718600 | tf_op jit(solution)/shard_map/ppermute | solution.py:18
  19.2 40.4 %copy-start.3 = (f32[6,32,128]{2,1,0:T(8,128)S(1)}, f32[6,32,128]{2,1,0:T(8,128)}, u32[]{:S(2)}) copy-start(f32[6,32,128]{2,1,0:T(8,128)} %param.5) | copy-start | bytes 294916
  124.5 51.6 %copy-start.1 = (bf16[64,6,32,128]{3,2,1,0:T(8,128)(2,1)S(1)}, bf16[64,6,32,128]{3,2,1,0:T(8,128)(2,1)}, u32[]{:S(2)}) copy-start(bf16[64,6,32,128]{3,2,1,0:T(8,128)(2,1)} %param.4) | copy-start | bytes 9437188
  176.2 9.3 %copy-start.2 = (bf16[64,24576]{1,0:T(8,128)(2,1)S(1)}, bf16[64,24576]{1,0:T(8,128)(2,1)}, u32[]{:S(2)}) copy-start(bf16[64,24576]{1,0:T(8,128)(2,1)} %convert_element_type.57) | copy-start | bytes 9437188
  874.0 9.0 %copy-start.4 = (f32[64,256]{1,0:T(8,128)}, f32[64,256]{1,0:T(8,128)S(1)}, u32[]{:S(2)}) copy-start(f32[64,256]{1,0:T(8,128)S(1)} %get-tuple-element.81) | copy-start | bytes 196612
  874.0 9.0 %copy-start.5 = (f32[64,256]{1,0:T(8,128)}, f32[64,256]{1,0:T(8,128)S(1)}, u32[]{:S(2)}) copy-start(f32[64,256]{1,0:T(8,128)S(1)} %get-tuple-element.82) | copy-start | bytes 196612
Sparse Core Ops, SparseCore 0:
  13.0 163.1 all-gather.1
  194.7 678.3 all-reduce.3
where the time goes:
time: 890 us
  waiting for transfers between devices  761 us (86%)
  local copies, waits for them, and re-layouts  48.4 us (5%)
  other arithmetic  45.8 us (5%)
  matrix products  18.4 us (2%)
  between operations  14.1 us (2%)
    psum x1, waiting for transfers between devices, body(): s_summed, h_summed = lax.psum((s_rows, h_rows), 'grid')  678 us
    all_gather x1, waiting for transfers between devices, body(): panel_rows = lax.all_gather(flat_psi, 'band', axis=0, tiled=True)  46.6 us
    ppermute x1, waiting for transfers between devices, padded_2(): lax.ppermute(tail, axis, [(i, (i + 1) % count) for i in range(count)])  34.2 us
    dynamic_update_slice x4, other arithmetic, body(): lax.map(lambda group: apply_hamiltonian(group, potential), groups)  26.6 us
    slice x24, local copies, waits for them, and re-layouts, apply_hamiltonian(): pair_y = jnp.roll(center, shift_by, 3) + jnp.roll(center, -shift_by, 3)  25.2 us
    dot_general x2, matrix products, row_products(): lax.dot_general(left, right, (((1,), (1,)), ((), ())), preferred_element_...  18.4 us
  transfers between devices with their start and end apart: 4, of which 4 were waited for; matrix products, arithmetic and copies ran while one was open for 9% of the time, Pallas kernels for 0%

commit v1 on v0

--- a/solution.py
+++ b/solution.py
@@ -1,9 +1,13 @@
+import functools
 import jax
 import jax.numpy as jnp
 from jax import lax
+from jax.experimental import pallas as pl
+from jax.experimental.pallas import tpu as pltpu
 from jax.sharding import PartitionSpec as P
 
 COEFFS = (-49.0 / 18.0, 3.0 / 2.0, -3.0 / 20.0, 1.0 / 90.0)
+MESH = pl.DeviceIdType.MESH
 
 
 def padded_2(cells, sides, width):
@@ -50,6 +54,100 @@
     )
 
 
+STRIDES = (1, 16, 4)
+SIDE = 4
+
+
+def grid_sum_kernel(v_ref, o_ref, bx, by, bz, qx, gy, gx, send_sem, recv_sem):
+    me = lax.axis_index("grid")
+    band = lax.axis_index("band")
+    rows = v_ref.shape[0]
+    rows_x, rows_y = rows // SIDE, rows // SIDE // SIDE
+    coord = [lax.rem(lax.div(me, s), SIDE) for s in STRIDES]
+
+    def peer(axis, d):
+        other = lax.rem(coord[axis] + d, SIDE)
+        return other, (band, me + (other - coord[axis]) * STRIDES[axis])
+
+    barrier = pltpu.get_barrier_semaphore()
+    for axis in range(3):
+        for d in range(1, SIDE):
+            pl.semaphore_signal(barrier, inc=1, device_id=peer(axis, d)[1], device_id_type=MESH)
+    pl.semaphore_wait(barrier, 3 * (SIDE - 1))
+
+    def exchange(phase, axis, source, landing):
+        mine = coord[axis]
+        copies = []
+        for d in range(1, SIDE):
+            other, device = peer(axis, d)
+            copy = pltpu.make_async_remote_copy(
+                src_ref=source(other),
+                dst_ref=landing(mine),
+                send_sem=send_sem.at[phase, d],
+                recv_sem=recv_sem.at[phase, d],
+                device_id=device,
+                device_id_type=MESH,
+            )
+            copy.start()
+            copies.append(copy)
+        return copies
+
+    def finish(copies):
+        for copy in copies:
+            copy.wait()
+
+    def piece(ref, n):
+        return lambda c: ref.at[pl.ds(pl.multiple_of(c * n, n), n)]
+
+    copies = exchange(0, 0, piece(v_ref, rows_x), lambda c: bx.at[c])
+    bx[coord[0]] = v_ref[pl.ds(pl.multiple_of(coord[0] * rows_x, rows_x), rows_x)]
+    finish(copies)
+    qx[...] = (bx[0] + bx[1]) + (bx[2] + bx[3])
+
+    copies = exchange(1, 1, piece(qx, rows_y), lambda c: by.at[c])
+    by[coord[1]] = qx[pl.ds(pl.multiple_of(coord[1] * rows_y, rows_y), rows_y)]
+    finish(copies)
+    bz[coord[2]] = (by[0] + by[1]) + (by[2] + by[3])
+
+    copies = exchange(2, 2, lambda c: bz.at[coord[2]], lambda c: bz.at[c])
+    finish(copies)
+    gy[coord[1]] = (bz[0] + bz[1]) + (bz[2] + bz[3])
+
+    copies = exchange(3, 1, lambda c: gy.at[coord[1]], lambda c: gy.at[c])
+    finish(copies)
+    gx[coord[0]] = gy[...].reshape(rows_x, gy.shape[-1])
+
+    copies = exchange(4, 0, lambda c: gx.at[coord[0]], lambda c: gx.at[c])
+    finish(copies)
+    o_ref[...] = gx[...].reshape(o_ref.shape)
+
+
+def grid_sum(v, collective_id):
+    rows, cols = v.shape
+    rows_x, rows_y = rows // SIDE, rows // SIDE // SIDE
+    f32 = jnp.float32
+    return pl.pallas_call(
+        grid_sum_kernel,
+        out_shape=jax.ShapeDtypeStruct(v.shape, f32),
+        in_specs=[pl.BlockSpec(memory_space=pltpu.VMEM)],
+        out_specs=pl.BlockSpec(memory_space=pltpu.VMEM),
+        scratch_shapes=[
+            pltpu.VMEM((SIDE, rows_x, cols), f32),
+            pltpu.VMEM((SIDE, rows_y, cols), f32),
+            pltpu.VMEM((SIDE, rows_y, cols), f32),
+            pltpu.VMEM((rows_x, cols), f32),
+            pltpu.VMEM((SIDE, rows_y, cols), f32),
+            pltpu.VMEM((SIDE, rows_x, cols), f32),
+            pltpu.SemaphoreType.DMA((5, SIDE)),
+            pltpu.SemaphoreType.DMA((5, SIDE)),
+        ],
+        compiler_params=pltpu.CompilerParams(
+            collective_id=collective_id, has_side_effects=True, vmem_limit_bytes=4 << 20
+        ),
+        name="grid_sum",
+    )(v)
+
+
 def body(orbitals, potential):
     shape = orbitals.shape
     orb_dev = shape[0]
@@ -64,8 +162,10 @@
     panel_rows = lax.all_gather(flat_psi, "band", axis=0, tiled=True)
     s_rows = row_products(flat_psi, panel_rows)
     h_rows = row_products(flat_h, panel_rows)
-    s_rows, h_rows = (s_rows, h_rows)
-    s_summed, h_summed = lax.psum((s_rows, h_rows), "grid")
+    columns = s_rows.shape[1]
+    summed = grid_sum(jnp.concatenate([s_rows, h_rows], 0).reshape(-1, 128), 1)
+    summed = summed.reshape(2 * orb_dev, columns)
+    s_summed, h_summed = summed[:orb_dev], summed[orb_dev:]
     intersection = s_summed / cell_count
     subspace = h_summed / cell_count
     offset_rows = lax.axis_index("band") * orb_dev

time: 890 us -> 278 us (0.31)
  waiting for transfers between devices: 761 us -> 82 us
  Pallas kernels: 0 us -> 68 us
    psum x1 -> x0, waiting for transfers between devices: 678 us -> none  [body(): s_summed, h_summed = lax.psum((s_rows, h_rows), 'grid')]
    pallas_call x0 -> x1, Pallas kernels: none -> 68 us  [grid_sum(): pl.pallas_call(grid_sum_kernel, out_shape=jax.ShapeDtypeStruct(v.shape, f...]
  transfers between devices with their start and end apart: 4 -> 3, of which waited for: 4 -> 3; matrix products, arithmetic and copies ran while one was open for 9% -> 28% of each run, Pallas kernels for 0% -> 0%
where the time goes in v1:
time: 278 us; the launch traced here: 277 us
  waiting for transfers between devices  82 us (29%)
  Pallas kernels  68 us (24%)
  local copies, waits for them, and re-layouts  48.5 us (17%)
  other arithmetic  45 us (16%)
  matrix products  17.1 us (6%)
  between operations  14.1 us (5%)
    pallas_call x1, Pallas kernels, grid_sum(): pl.pallas_call(grid_sum_kernel, out_shape=jax.ShapeDtypeStruct(v.shape, f...  68 us
    all_gather x1, waiting for transfers between devices, body(): panel_rows = lax.all_gather(flat_psi, 'band', axis=0, tiled=True)  46.6 us
    ppermute x1, waiting for transfers between devices, padded_2(): lax.ppermute(tail, axis, [(i, (i + 1) % count) for i in range(count)])  34.2 us
    dynamic_update_slice x4, other arithmetic, body(): lax.map(lambda group: apply_hamiltonian(group, potential), groups)  26.6 us
    slice x24, local copies, waits for them, and re-layouts, apply_hamiltonian(): pair_y = jnp.roll(center, shift_by, 3) + jnp.roll(center, -shift_by, 3)  25.2 us
    dot_general x2, matrix products, row_products(): lax.dot_general(left, right, (((1,), (1,)), ((), ())), preferred_element_...  17.1 us
    unnamed x13, local copies, waits for them, and re-layouts  7.51 us
    div x1, other arithmetic, body(): (hpsi - rayleigh[:, None, None, None] * orbitals.astype(jnp.float32)) / (...  7.19 us
  transfers between devices with their start and end apart: 3, of which 3 were waited for; matrix products, arithmetic and copies ran while one was open for 28% of the time, Pallas kernels for 0%

profile of v1, /device:TPU:2, one launch (start us, length us, event | category | flops | bytes accessed | tf_op | source)
XLA Modules:
  0.0 277.2 jit_solution(1649944173014591072)
XLA Ops:
  7.2 5.6 %copy.8 = bf16[8,8,192,128]{3,1,2,0:T(8,128)(2,1)} copy(bf16[8,8,192,128]{3,2,1,0:T(8,128)(2,1)} %bitcast.28) | data formatting | bytes 6291456
  12.9 1.9 copy-done
  14.7 2.3 fusion.27
  19.3 34.2 %collective-permute-done = bf16[64,3,32,128]{3,2,1,0:T(8,128)(2,1)} collective-permute-done((bf16[64,3,32,128]{3,2,1,0:T(8,128)(2,1)}, bf16[64,3,32,128]{3,2,1,0:T(8,128)(2,1)}, u32[]{:S(2)}, u32[]{:S(2)}) %collective-permute-start) | collective-permute-done | bytes 1572896 | tf_op jit(solution)/shard_map/ppermute | solution.py:20
  54.6 5.0 %pad_maximum_fusion = bf16[64,12,32,128]{3,2,1,0:T(8,128)(2,1)} fusion(bf16[64,3,32,128]{3,2,1,0:T(8,128)(2,1)} %collective-permute-done.1, bf16[64,6,32,128]{3,2,1,0:T(8,128)(2,1)S(1)} %copy-done, bf16[64,3,32,128]{3,2,1,0:T(8,128)(2,1)} %collective-permute-done), kind=kLoop, calls=%fused_computation.32 | loop fusion | flops 6291456 | bytes 12582912 | tf_op jit(solution)/shard_map/concatenate | solution.py:18
  59.6 59.5 %while.12 = (s32[]{:T(128)}, f32[4,16,6,32,128]{4,3,2,1,0:T(8,128)}, bf16[4,16,12,32,128]{4,3,2,1,0:T(8,128)(2,1)}, f32[6,32,128]{2,1,0:T(8,128)S(1)}, s32[]{:T(128)}) while((s32[]{:T(128)}, f32[4,16,6,32,128]{4,3,2,1,0:T(8,128)}, bf16[4,16,12,32,128]{4,3,2,1,0:T(8,128)(2,1)}, f32[6,32,128]{2,1,0:T(8,128)S(1)}, s32[]{:T(128)}) %tuple.57), condition=%wide.region_1.2_spmd, body=%wide.region_0.1_spmd.sunk | while | flops 14942210 | bytes 44888640 | solution.py:159
  63.9 1.7 fusion.43
  65.6 2.2 fusion.44
  67.9 6.7 %fusion.45 = f32[4,16,6,32,128]{4,3,2,1,0:T(8,128)} fusion(f32[4,16,6,32,128]{4,3,2,1,0:T(8,128)} %get-tuple-element.138, s32[]{:T(128)} %get-tuple-element.137, f32[16,6,32,128]{3,2,1,0:T(8,128)S(1)} %slice_convert_fusion.2, f32[16,6,32,127]{3,2,1,0:T(8,128)S(1)} %get-tuple-element.120, f32[16,6,32,1]{3,2,1,0:T(8,128)S(1)} %get-tuple-element.121, ...), kind=kLoop, calls=%fused_computation.18.clone.1 | loop fusion | flops 14548992 | bytes 20509184 | tf_op jit(solution)/shard_map/while/body/jit(dynamic_update_index_in_dim)/dynamic_update_slice | solution.py:159
  78.8 1.7 fusion.43
  80.5 2.3 fusion.44
  82.8 6.6 %fusion.45 = f32[4,16,6,32,128]{4,3,2,1,0:T(8,128)} fusion(f32[4,16,6,32,128]{4,3,2,1,0:T(8,128)} %get-tuple-element.138, s32[]{:T(128)} %get-tuple-element.137, f32[16,6,32,128]{3,2,1,0:T(8,128)S(1)} %slice_convert_fusion.2, f32[16,6,32,127]{3,2,1,0:T(8,128)S(1)} %get-tuple-element.120, f32[16,6,32,1]{3,2,1,0:T(8,128)S(1)} %get-tuple-element.121, ...), kind=kLoop, calls=%fused_computation.18.clone.1 | loop fusion | flops 14548992 | bytes 20509184 | tf_op jit(solution)/shard_map/while/body/jit(dynamic_update_index_in_dim)/dynamic_update_slice | solution.py:159
  95.4 2.2 fusion.44
  97.6 6.8 %fusion.45 = f32[4,16,6,32,128]{4,3,2,1,0:T(8,128)} fusion(f32[4,16,6,32,128]{4,3,2,1,0:T(8,128)} %get-tuple-element.138, s32[]{:T(128)} %get-tuple-element.137, f32[16,6,32,128]{3,2,1,0:T(8,128)S(1)} %slice_convert_fusion.2, f32[16,6,32,127]{3,2,1,0:T(8,128)S(1)} %get-tuple-element.120, f32[16,6,32,1]{3,2,1,0:T(8,128)S(1)} %get-tuple-element.121, ...), kind=kLoop, calls=%fused_computation.18.clone.1 | loop fusion | flops 14548992 | bytes 20509184 | tf_op jit(solution)/shard_map/while/body/jit(dynamic_update_index_in_dim)/dynamic_update_slice | solution.py:159
  108.6 1.7 fusion.43
  110.4 2.2 fusion.44
  112.6 6.6 %fusion.45 = f32[4,16,6,32,128]{4,3,2,1,0:T(8,128)} fusion(f32[4,16,6,32,128]{4,3,2,1,0:T(8,128)} %get-tuple-element.138, s32[]{:T(128)} %get-tuple-element.137, f32[16,6,32,128]{3,2,1,0:T(8,128)S(1)} %slice_convert_fusion.2, f32[16,6,32,127]{3,2,1,0:T(8,128)S(1)} %get-tuple-element.120, f32[16,6,32,1]{3,2,1,0:T(8,128)S(1)} %get-tuple-element.121, ...), kind=kLoop, calls=%fused_computation.18.clone.1 | loop fusion | flops 14548992 | bytes 20509184 | tf_op jit(solution)/shard_map/while/body/jit(dynamic_update_index_in_dim)/dynamic_update_slice | solution.py:159
  119.2 5.3 %convert_element_type.56 = bf16[4,16,6,32,128]{4,3,2,1,0:T(8,128)(2,1)} convert(f32[4,16,6,32,128]{4,3,2,1,0:T(8,128)} %get-tuple-element.56) | non-fusion elementwise | flops 1572864 | bytes 9437184 | tf_op jit(solution)/shard_map/convert_element_type | solution.py:161
  124.5 5.0 %convert_element_type.57 = bf16[64,24576]{1,0:T(8,128)(2,1)} reshape(bf16[4,16,6,32,128]{4,3,2,1,0:T(8,128)(2,1)} %convert_element_type.56) | data formatting | bytes 6291456 | tf_op jit(solution)/shard_map/convert_element_type | solution.py:161
  129.5 46.6 %all-gather.2.cloned.1.call-done = bf16[256,24576]{1,0:T(8,128)(2,1)} async-done(((bf16[64,24576]{1,0:T(8,128)(2,1)}), bf16[256,24576]{1,0:T(8,128)(2,1)}) %all-gather.2.cloned.1.call-update) | async-done | bytes 12582928 | tf_op jit(solution)/shard_map/all_gather | solution.py:162
  176.2 8.7 %fusion.20 = f32[64,256]{1,0:T(8,128)S(1)} fusion(bf16[256,24576]{1,0:T(8,128)(2,1)} %all-gather.2.cloned.1.call-done, bf16[8,8,192,128]{3,2,1,0:T(8,128)(2,1)S(1)} %bitcast.29), kind=kOutput, calls=%fused_computation.44 | convolution fusion | flops 805306368 | bytes 15794176 | tf_op jit(solution)/shard_map/dot_general | solution.py:52
  184.8 8.5 %fusion.28 = f32[64,256]{1,0:T(8,128)S(1)} fusion(bf16[64,24576]{1,0:T(8,128)(2,1)S(1)} %copy-done.2, bf16[256,24576]{1,0:T(8,128)(2,1)} %all-gather.2.cloned.1.call-done), kind=kOutput, calls=%fused_computation.52 | convolution fusion | flops 805306368 | bytes 15794176 | tf_op jit(solution)/shard_map/dot_general | solution.py:52
  193.4 68.0 %grid_sum.1 = f32[256,128]{1,0:T(8,128)S(1)} custom-call(f32[256,128]{1,0:T(8,128)S(1)} %reshape.39.v_ref), custom_call_target="tpu_custom_call" | custom-call | tf_op jit(solution)/shard_map/grid_sum/pallas_call | solution.py:129
  263.2 7.2 %fusion.19 = f32[64,6,32,128]{3,2,1,0:T(8,128)} fusion(f32[4,16,6,32,128]{4,3,2,1,0:T(8,128)} %get-tuple-element.56, bf16[64,6,32,128]{3,2,1,0:T(8,128)(2,1)S(1)} %copy-done.1, f32[6,32,128]{2,1,0:T(8,128)S(1)} %broadcast_add_fusion, f32[64]{0:T(128)S(1)} %add_divide_fusion), kind=kLoop, calls=%fused_computation.34 | loop fusion | flops 6291456 | bytes 15827200 | tf_op jit(solution)/shard_map/div | solution.py:175
  (53 shorter events, 23.9 us)
Async XLA Ops:
  7.2 169.0 %all-gather.2.cloned.1.call-start = ((), (), s32[]{:S(2)}) async-start(), calls=%async_computation | async-start | bytes 15728640 | tf_op jit(solution)/shard_map/all_gather | solution.py:162
  12.8 1.9 copy-start
  14.7 4.5 %copy-start.3 = (f32[6,32,128]{2,1,0:T(8,128)S(1)}, f32[6,32,128]{2,1,0:T(8,128)}, u32[]{:S(2)}) copy-start(f32[6,32,128]{2,1,0:T(8,128)} %param.5) | copy-start | bytes 294916
  17.0 36.5 %collective-permute-start = (bf16[64,3,32,128]{3,2,1,0:T(8,128)(2,1)}, bf16[64,3,32,128]{3,2,1,0:T(8,128)(2,1)}, u32[]{:S(2)}, u32[]{:S(2)}) collective-permute-start(bf16[64,3,32,128]{3,2,1,0:T(8,128)(2,1)} %get-tuple-element.77), channel_id=1, source_target_pairs={{0,1},{1,2},{2,3},{3,4},{4,5},{5,6},{6,7},{7,8},{8,9},{9,10},{10,1... | collective-permute-start | bytes 4718600 | tf_op jit(solution)/shard_map/ppermute | solution.py:20
  18.5 36.2 %collective-permute-start.1 = (bf16[64,3,32,128]{3,2,1,0:T(8,128)(2,1)}, bf16[64,3,32,128]{3,2,1,0:T(8,128)(2,1)}, u32[]{:S(2)}, u32[]{:S(2)}) collective-permute-start(bf16[64,3,32,128]{3,2,1,0:T(8,128)(2,1)} %get-tuple-element.78), channel_id=1, source_target_pairs={{1,0},{2,1},{3,2},{4,3},{5,4},{6,5},{7,6},{8,7},{9,8},{10,9},{11,1... | collective-permute-start | bytes 4718600 | tf_op jit(solution)/shard_map/ppermute | solution.py:22
  124.5 51.7 %copy-start.1 = (bf16[64,6,32,128]{3,2,1,0:T(8,128)(2,1)S(1)}, bf16[64,6,32,128]{3,2,1,0:T(8,128)(2,1)}, u32[]{:S(2)}) copy-start(bf16[64,6,32,128]{3,2,1,0:T(8,128)(2,1)} %param.4) | copy-start | bytes 9437188
  176.2 8.7 %copy-start.2 = (bf16[64,24576]{1,0:T(8,128)(2,1)S(1)}, bf16[64,24576]{1,0:T(8,128)(2,1)}, u32[]{:S(2)}) copy-start(bf16[64,24576]{1,0:T(8,128)(2,1)} %convert_element_type.57) | copy-start | bytes 9437188
  261.4 9.0 %copy-start.4 = (f32[64,256]{1,0:T(8,128)}, f32[64,256]{1,0:T(8,128)S(1)}, u32[]{:S(2)}) copy-start(f32[64,256]{1,0:T(8,128)S(1)} %div.26) | copy-start | bytes 196612
  261.4 8.9 %copy-start.5 = (f32[64,256]{1,0:T(8,128)}, f32[64,256]{1,0:T(8,128)S(1)}, u32[]{:S(2)}) copy-start(f32[64,256]{1,0:T(8,128)S(1)} %div.28) | copy-start | bytes 196612
Sparse Core Ops, SparseCore 0:
  13.0 163.1 all-gather.1

commit v2 on v1

v2 whole, which is shorter than its diff:
```python
import jax
import jax.numpy as jnp
from jax import lax
from jax.experimental import pallas as pl
from jax.experimental.pallas import tpu as pltpu
from jax.sharding import PartitionSpec as P

COEFFS = (-49.0 / 18.0, 3.0 / 2.0, -3.0 / 20.0, 1.0 / 90.0)
HALVED = tuple(-0.5 * c for c in COEFFS)
REACH = len(COEFFS) - 1
MESH = pl.DeviceIdType.MESH
F32 = jnp.float32
BF16 = jnp.bfloat16

CUT = 18
WINDOW = 18


def upper_chip():
    return lax.div(lax.axis_index("band"), 2)


STRIDES = (1, 16, 4)
SIDE = 4


def grid_sum_kernel(v_ref, o_ref, bx, by, bz, qx, gy, gx, send_sem, recv_sem):
    me = lax.axis_index("grid")
    band = lax.axis_index("band")
    rows = v_ref.shape[0]
    rows_x, rows_y = rows // SIDE, rows // SIDE // SIDE
    coord = [lax.rem(lax.div(me, s), SIDE) for s in STRIDES]

    def peer(axis, d):
        other = lax.rem(coord[axis] + d, SIDE)
        return other, (band, me + (other - coord[axis]) * STRIDES[axis])

    barrier = pltpu.get_barrier_semaphore()
    for axis in range(3):
        for d in range(1, SIDE):
            pl.semaphore_signal(barrier, inc=1, device_id=peer(axis, d)[1], device_id_type=MESH)
    pl.semaphore_wait(barrier, 3 * (SIDE - 1))

    def exchange(phase, axis, source, landing):
        mine = coord[axis]
        copies = []
        for d in range(1, SIDE):
            other, device = peer(axis, d)
            copy = pltpu.make_async_remote_copy(
                src_ref=source(other),
                dst_ref=landing(mine),
                send_sem=send_sem.at[phase, d],
                recv_sem=recv_sem.at[phase, d],
                device_id=device,
                device_id_type=MESH,
            )
            copy.start()
            copies.append(copy)
        return copies

    def finish(copies):
        for copy in copies:
            copy.wait()

    def piece(ref, n):
        return lambda c: ref.at[pl.ds(pl.multiple_of(c * n, n), n)]

    copies = exchange(0, 0, piece(v_ref, rows_x), lambda c: bx.at[c])
    bx[coord[0]] = v_ref[pl.ds(pl.multiple_of(coord[0] * rows_x, rows_x), rows_x)]
    finish(copies)
    qx[...] = (bx[0] + bx[1]) + (bx[2] + bx[3])

    copies = exchange(1, 1, piece(qx, rows_y), lambda c: by.at[c])
    by[coord[1]] = qx[pl.ds(pl.multiple_of(coord[1] * rows_y, rows_y), rows_y)]
    finish(copies)
    bz[coord[2]] = (by[0] + by[1]) + (by[2] + by[3])

    copies = exchange(2, 2, lambda c: bz.at[coord[2]], lambda c: bz.at[c])
    finish(copies)
    gy[coord[1]] = (bz[0] + bz[1]) + (bz[2] + bz[3])

    copies = exchange(3, 1, lambda c: gy.at[coord[1]], lambda c: gy.at[c])
    finish(copies)
    gx[coord[0]] = gy[...].reshape(rows_x, gy.shape[-1])

    copies = exchange(4, 0, lambda c: gx.at[coord[0]], lambda c: gx.at[c])
    finish(copies)
    o_ref[...] = gx[...].reshape(o_ref.shape)


def grid_sum(v, collective_id):
    rows, cols = v.shape
    rows_x, rows_y = rows // SIDE, rows // SIDE // SIDE
    return pl.pallas_call(
        grid_sum_kernel,
        out_shape=jax.ShapeDtypeStruct(v.shape, F32),
        in_specs=[pl.BlockSpec(memory_space=pltpu.VMEM)],
        out_specs=pl.BlockSpec(memory_space=pltpu.VMEM),
        scratch_shapes=[
            pltpu.VMEM((SIDE, rows_x, cols), F32),
            pltpu.VMEM((SIDE, rows_y, cols), F32),
            pltpu.VMEM((SIDE, rows_y, cols), F32),
            pltpu.VMEM((rows_x, cols), F32),
            pltpu.VMEM((SIDE, rows_y, cols), F32),
            pltpu.VMEM((SIDE, rows_x, cols), F32),
            pltpu.SemaphoreType.DMA((5, SIDE)),
            pltpu.SemaphoreType.DMA((5, SIDE)),
        ],
        compiler_params=pltpu.CompilerParams(
            collective_id=collective_id, has_side_effects=True, vmem_limit_bytes=4 << 20
        ),
        name="grid_sum",
    )(v)


def stencil_kernel(psi_ref, lo_ref, hi_ref, v_ref, hpsi_ref, half_ref, g_ref, field):
    layers, planes = psi_ref.shape[:2]

    @pl.when(pl.program_id(0) == 0)
    def _():
        edge = jnp.zeros((layers + 2 * REACH, REACH) + psi_ref.shape[2:], F32)
        field[:, :REACH] = edge
        field[:, REACH + planes :] = edge

    @pl.loop(0, planes)
    def _(z):
        for x in range(REACH):
            field[x, z + REACH] = lo_ref[x, z].astype(F32)
            field[x + REACH + layers, z + REACH] = hi_ref[x, z].astype(F32)
        for x in range(layers):
            field[x + REACH, z + REACH] = psi_ref[x, z].astype(F32)

    @pl.loop(0, planes)
    def _(z):
        for x in range(layers):
            i, j = x + REACH, z + REACH
            center = field[i, j]
            total = (3.0 * HALVED[0] + v_ref[x, pl.ds(z, 1), :]) * center
            for k in range(1, REACH + 1):
                pair_x = field[i + k, j] + field[i - k, j]
                pair_z = field[i, j + k] + field[i, j - k]
                pair_y = pltpu.roll(center, k, 1) + pltpu.roll(center, center.shape[1] - k, 1)
                total = total + HALVED[k] * (pair_x + pair_z + pair_y)
            hpsi_ref[x, z] = total
            half_ref[x, z] = total.astype(BF16)

    upper = upper_chip()
    first = upper * (planes - WINDOW)
    for x in range(layers):
        for i in range(WINDOW):
            g_ref[x, i] = half_ref[x, first + i]

    @pl.when(upper == 1)
    def _():
        for x in range(layers):
            for z in range(planes - WINDOW, CUT + REACH):
                if z < CUT:
                    total = jnp.zeros(psi_ref.shape[2:], F32)
                    for k in range(CUT - z, REACH + 1):
                        total = total + HALVED[k] * field[x + REACH, z + REACH + k]
                else:
                    total = hpsi_ref[x, z]
                    for k in range(z - CUT + 1, REACH + 1):
                        total = total - HALVED[k] * field[x + REACH, z + REACH - k]
                g_ref[x, z - (planes - WINDOW)] = total.astype(BF16)


def stencil(psi, lo, hi, potential):
    layers, planes, orbs, ny = psi.shape
    block = 16

    def spec(n, m):
        return pl.BlockSpec((n, m, block, ny), lambda o: (0, 0, o, 0))

    return pl.pallas_call(
        stencil_kernel,
        grid=(orbs // block,),
        out_shape=(
            jax.ShapeDtypeStruct(psi.shape, F32),
            jax.ShapeDtypeStruct(psi.shape, BF16),
            jax.ShapeDtypeStruct((layers, WINDOW, orbs, ny), BF16),
        ),
        in_specs=[
            spec(layers, planes),
            spec(REACH, planes),
            spec(REACH, planes),
            pl.BlockSpec(potential.shape, lambda o: (0, 0, 0)),
        ],
        out_specs=(spec(layers, planes), spec(layers, planes), spec(layers, WINDOW)),
        scratch_shapes=[pltpu.VMEM((layers + 2 * REACH, planes + 2 * REACH, block, ny), F32)],
        compiler_params=pltpu.CompilerParams(vmem_limit_bytes=40 << 20),
        cost_estimate=pl.CostEstimate(flops=int(4e9), bytes_accessed=int(30e6), transcendentals=0),
        name="stencil",
    )(psi, lo, hi, potential)


def contract(left, right):
    return lax.dot_general(left, right, (((1,), (1,)), ((), ())), preferred_element_type=F32)


def chip_kernel(psi_ref, half_ref, par_ref, o_ref):
    @pl.when(pl.program_id(0) == 0)
    def _():
        o_ref[...] = jnp.zeros_like(o_ref)

    planes = psi_ref.shape[1]
    group = 8
    for z in range(0, planes, group):
        def wide(ref):
            return jnp.concatenate([ref[0, z + i] for i in range(group)], axis=1)

        psi = wide(psi_ref)
        left = jnp.concatenate([psi, wide(half_ref)], axis=0)
        right = jnp.concatenate([psi, wide(par_ref)], axis=0)
        o_ref[...] += contract(left, right)


def chip_products(psi, half, par):
    layers, planes, orbs, ny = psi.shape
    spec = pl.BlockSpec((1, planes, orbs, ny), lambda x: (x, 0, 0, 0))
    return pl.pallas_call(
        chip_kernel,
        grid=(layers,),
        out_shape=jax.ShapeDtypeStruct((2 * orbs, 2 * orbs), F32),
        in_specs=[spec, spec, spec],
        out_specs=pl.BlockSpec((2 * orbs, 2 * orbs), lambda x: (0, 0)),
        compiler_params=pltpu.CompilerParams(vmem_limit_bytes=24 << 20),
        cost_estimate=pl.CostEstimate(flops=int(1e9), bytes_accessed=int(9.5e6), transcendentals=0),
        name="chip_products",
    )(psi, half, par)


def cross_kernel(psi_ref, par_ref, g_ref, gpar_ref, far_ref, o_ref, acc):
    @pl.when(pl.program_id(0) == 0)
    def _():
        acc[...] = jnp.zeros_like(acc)

    planes = psi_ref.shape[1]
    upper = upper_chip()
    first = upper * (planes - WINDOW)
    keep = (1 - upper).astype(F32).astype(BF16)
    skipped = CUT - (planes - WINDOW)
    group = 6
    for z in range(0, WINDOW, group):
        def wide(ref, offset, masked):
            parts = [ref[0, offset + z + i] for i in range(group)]
            if masked:
                parts = [p * keep if z + i < skipped else p for i, p in enumerate(parts)]
            return jnp.concatenate(parts, axis=1)

        left = jnp.concatenate(
            [
                wide(psi_ref, first, True),
                wide(par_ref, first, True),
                wide(g_ref, 0, False),
                wide(gpar_ref, 0, False),
            ],
            axis=0,
        )
        acc[...] += contract(left, wide(far_ref, 0, False))

    @pl.when(pl.program_id(0) == pl.num_programs(0) - 1)
    def _():
        rows = acc.shape[0] // 2
        o_ref[...] = jnp.concatenate([acc[:rows], acc[rows:]], axis=1)


def cross_products(psi, par, g, g_par, far):
    layers, planes, orbs, ny = psi.shape
    whole = pl.BlockSpec((1, planes, orbs, ny), lambda x: (x, 0, 0, 0))
    part = pl.BlockSpec((1, WINDOW, orbs, ny), lambda x: (x, 0, 0, 0))
    return pl.pallas_call(
        cross_kernel,
        grid=(layers,),
        out_shape=jax.ShapeDtypeStruct((2 * orbs, 2 * orbs), F32),
        in_specs=[whole, whole, part, part, part],
        out_specs=pl.BlockSpec((2 * orbs, 2 * orbs), lambda x: (0, 0)),
        scratch_shapes=[pltpu.VMEM((4 * orbs, orbs), F32)],
        compiler_params=pltpu.CompilerParams(vmem_limit_bytes=24 << 20),
        cost_estimate=pl.CostEstimate(flops=int(1e9), bytes_accessed=int(11e6), transcendentals=0),
        name="cross_products",
    )(psi, par, g, g_par, far)


def gradient_kernel(cells, hpsi_ref, psi_ref, v_ref, sums_ref, o_ref, ray):
    orbs = o_ref.shape[0]

    @pl.when((pl.program_id(0) == 0) & (pl.program_id(1) == 0))
    def _():
        shape = (orbs, orbs)
        same = lax.broadcasted_iota(jnp.int32, shape, 0) == lax.broadcasted_iota(jnp.int32, shape, 1)

        def diagonal(rows):
            picked = jnp.where(same, sums_ref[rows : rows + orbs, :orbs], 0.0)
            return jnp.sum(picked, axis=1, keepdims=True) / cells

        ray[...] = jnp.broadcast_to(diagonal(orbs) / (diagonal(0) + 1e-06), ray.shape)

    rayleigh = ray[...]
    v = v_ref[0]
    parts = []
    for z in range(hpsi_ref.shape[1]):
        parts.append(
            (hpsi_ref[0, z] - rayleigh * psi_ref[0, z].astype(F32)) / (2.0 + v[z : z + 1])
        )
    o_ref[:, 0] = jnp.swapaxes(jnp.stack(parts, axis=0), 0, 1)


def gradient_of(hpsi, psi, potential, sums, cells):
    layers, planes, orbs, ny = psi.shape
    block = 8
    spec = pl.BlockSpec((1, block, orbs, ny), lambda x, z: (x, z, 0, 0))
    return pl.pallas_call(
        lambda *refs: gradient_kernel(cells, *refs),
        grid=(layers, planes // block),
        out_shape=jax.ShapeDtypeStruct((orbs, layers, planes, ny), F32),
        in_specs=[
            spec,
            spec,
            pl.BlockSpec((1, block, ny), lambda x, z: (x, z, 0)),
            pl.BlockSpec(sums.shape, lambda x, z: (0, 0)),
        ],
        out_specs=pl.BlockSpec((orbs, 1, block, ny), lambda x, z: (0, x, z, 0)),
        scratch_shapes=[pltpu.VMEM((orbs, ny), F32)],
        compiler_params=pltpu.CompilerParams(vmem_limit_bytes=16 << 20),
        cost_estimate=pl.CostEstimate(flops=int(1e7), bytes_accessed=int(16e6), transcendentals=0),
        name="gradient",
    )(hpsi, psi, potential, sums)


def body(orbitals, potential):
    orbs, layers, planes, ny = orbitals.shape
    grids = lax.axis_size("grid")
    cells = layers * grids * planes * ny
    band = lax.axis_index("band")
    upper, core = lax.div(band, 2), lax.rem(band, 2)
    other_core = [(0, 1), (1, 0), (2, 3), (3, 2)]
    other_chip = [(0, 2), (1, 3), (2, 0), (3, 1)]

    psi = jnp.transpose(orbitals, (1, 2, 0, 3))
    wanted = lax.dynamic_slice_in_dim(psi, (1 - upper) * (planes - WINDOW), WINDOW, 1)
    far = lax.ppermute(wanted, "band", other_chip)
    lo = lax.ppermute(psi[layers - REACH :], "grid", [(i, (i + 1) % grids) for i in range(grids)])
    hi = lax.ppermute(psi[:REACH], "grid", [((i + 1) % grids, i) for i in range(grids)])
    par = lax.ppermute(psi, "band", other_core)

    hpsi, half, g = stencil(psi, lo, hi, potential)
    g_par = lax.ppermute(g, "band", other_core)
    chip = grid_sum(chip_products(psi, half, par), 1)
    gradient = gradient_of(hpsi, psi, potential, chip, cells)

    cross = grid_sum(cross_products(psi, par, g, g_par, far), 2)
    cross_par = lax.ppermute(cross[orbs:], "band", other_core)
    cross_far = lax.ppermute(cross, "band", other_chip)

    def rows_of(which):
        mine = chip[which * orbs : (which + 1) * orbs]
        columns = slice(which * orbs, (which + 1) * orbs)
        turned = cross_far[:, columns].T
        own = cross[:orbs, columns] + turned[:, :orbs]
        par_columns = cross_par[:, columns] + turned[:, orbs:]
        first, second = mine[:, :orbs], mine[:, orbs:]
        near = jnp.where(core == 0, jnp.concatenate([first, second], 1), jnp.concatenate([second, first], 1))
        away = jnp.where(
            core == 0, jnp.concatenate([own, par_columns], 1), jnp.concatenate([par_columns, own], 1)
        )
        rows = jnp.where(upper == 0, jnp.concatenate([near, away], 1), jnp.concatenate([away, near], 1))
        return rows / cells

    return (gradient, rows_of(0), rows_of(1))


def solution(mesh):
    in_specs = (P("band", "grid", None, None), P("grid", None, None))
    out_specs = (P("band", "grid", None, None), P("band", None), P("band", None))
    return jax.shard_map(body, mesh=mesh, in_specs=in_specs, out_specs=out_specs, check_vma=False)
```

time: 278 us -> 189 us (0.68)
  Pallas kernels: 68 us -> 127 us
  waiting for transfers between devices: 82 us -> 28.2 us
  other arithmetic: 45 us -> 1.56 us
  local copies, waits for them, and re-layouts: 48.5 us -> 15.6 us
  matrix products: 17.1 us -> 0 us
  between operations: 14.1 us -> 0.73 us
  starting transfers between devices: 2.28 us -> 12.9 us
    pallas_call x1 -> x6, Pallas kernels: 68 us -> 127 us  [the longest x2 82.8 us: grid_sum(): pl.pallas_call(grid_sum_kernel, out_shape=jax.ShapeDtypeStruct(v.shape, F...]
    all_gather x1 -> x0, waiting for transfers between devices: 46.6 us -> none  [body(): panel_rows = lax.all_gather(flat_psi, 'band', axis=0, tiled=True)]
    dynamic_update_slice x4 -> x0, other arithmetic: 26.6 us -> none  [body(): lax.map(lambda group: apply_hamiltonian(group, potential), groups)]
    slice x25 -> x3, local copies, waits for them, and re-layouts: 27.5 us -> 3.17 us  [the longest x1 3.09 us: body(): psi[:REACH]]
    dot_general x2 -> x0, matrix products: 17.1 us -> none  [row_products(): lax.dot_general(left, right, (((1,), (1,)), ((), ())), preferred_element_...]
    ppermute x2 -> x7, starting transfers between devices: 2.24 us -> 12.9 us  [the longest x1 6.97 us: body(): far = lax.ppermute(wanted, 'band', other_chip)]
    ppermute x2 -> x7, waiting for transfers between devices: 35.4 us -> 28.2 us  [the longest x1 25.8 us: body(): lax.ppermute(psi[layers - REACH:], 'grid', [(i, (i + 1) % grids) for i in...]
    squeeze x4 -> x0, local copies, waits for them, and re-layouts: 6.72 us -> none  [body(): lax.map(lambda group: apply_hamiltonian(group, potential), groups)]
  transfers between devices with their start and end apart: 3 -> 7, of which waited for: 3 -> 3; matrix products, arithmetic and copies ran while one was open for 28% -> 1% of each run, Pallas kernels for 0% -> 54%
where the time goes in v2:
time: 189 us; the launch traced here: 186 us
  Pallas kernels  127 us (67%)
  waiting for transfers between devices  28.2 us (15%)
  local copies, waits for them, and re-layouts  15.6 us (8%)
  starting transfers between devices  12.9 us (7%)
    pallas_call x2, Pallas kernels, grid_sum(): pl.pallas_call(grid_sum_kernel, out_shape=jax.ShapeDtypeStruct(v.shape, F...  82.8 us
    ppermute x1, waiting for transfers between devices, body(): lax.ppermute(psi[layers - REACH:], 'grid', [(i, (i + 1) % grids) for i in...  25.8 us
    pallas_call x1, Pallas kernels, stencil(): pl.pallas_call(stencil_kernel, grid=(orbs // block,), out_shape=(jax.Shap...  23.8 us
    unnamed x9, local copies, waits for them, and re-layouts  10.3 us
    pallas_call x1, Pallas kernels, gradient_of(): pl.pallas_call(lambda *refs: gradient_kernel(cells, *refs), grid=(layers,...  9.64 us
    ppermute x1, starting transfers between devices, body(): far = lax.ppermute(wanted, 'band', other_chip)  6.97 us
    pallas_call x1, Pallas kernels, cross_products(): pl.pallas_call(cross_kernel, grid=(layers,), out_shape=jax.ShapeDtypeStru...  6.15 us
    pallas_call x1, Pallas kernels, chip_products(): pl.pallas_call(chip_kernel, grid=(layers,), out_shape=jax.ShapeDtypeStruc...  4.99 us
  transfers between devices with their start and end apart: 7, of which 3 were waited for; matrix products, arithmetic and copies ran while one was open for 1% of the time, Pallas kernels for 54%

profile of v2, /device:TPU:2, one launch (start us, length us, event | category | flops | bytes accessed | tf_op | source)
XLA Modules:
  0.0 186.4 jit_solution(6932121113407774779)
XLA Ops:
  0.6 3.9 %copy.10 = bf16[64,6,32,128]{3,0,2,1:T(8,128)(2,1)S(1)} copy(bf16[64,6,32,128]{3,2,1,0:T(8,128)(2,1)} %param.2) | data formatting | bytes 6291456 | tf_op args[0]
  4.5 3.1 %fusion.3 = (bf16[3,32,64,128]{3,2,1,0:T(8,128)(2,1)}, bf16[3,32,64,128]{3,2,1,0:T(8,128)(2,1)}) fusion(bf16[6,32,64,128]{3,2,1,0:T(8,128)(2,1)S(1)} %bitcast.8), kind=kLoop, calls=%fused_computation.17 | loop fusion | bytes 6291456 | tf_op jit(solution)/shard_map/slice | solution.py:344
  7.6 1.5 collective-permute-start
  9.1 0.8 collective-permute-start.1
  9.9 1.4 dynamic-slice_bitcast_fusion
  11.3 7.0 %collective-permute-start.4 = (bf16[6,18,64,128]{3,2,1,0:T(8,128)(2,1)}, bf16[6,18,64,128]{3,2,1,0:T(8,128)(2,1)}, u32[]{:S(2)}, u32[]{:S(2)}) collective-permute-start(bf16[6,18,64,128]{3,2,1,0:T(8,128)(2,1)} %dynamic-slice_bitcast_fusion), channel_id=1, source_target_pairs={{0,128},{64,192},{128,0},{192,64},{1,129},{65,193},{129,1},{193,65... | collective-permute-start | bytes 5308424 | tf_op jit(solution)/shard_map/ppermute | solution.py:342
  18.3 25.8 %collective-permute-done.lo_ref = bf16[3,32,64,128]{3,2,1,0:T(8,128)(2,1)} collective-permute-done((bf16[3,32,64,128]{3,2,1,0:T(8,128)(2,1)}, bf16[3,32,64,128]{3,2,1,0:T(8,128)(2,1)}, u32[]{:S(2)}, u32[]{:S(2)}) %collective-permute-start) | collective-permute-done | bytes 1572896 | tf_op jit(solution)/shard_map/ppermute | solution.py:343
  44.1 1.2 collective-permute-done.1.hi_ref
  45.3 23.8 %stencil.1 = (f32[6,32,64,128]{3,2,1,0:T(8,128)}, bf16[6,32,64,128]{3,2,1,0:T(8,128)(2,1)S(1)}, bf16[6,18,64,128]{3,2,1,0:T(8,128)(2,1)}) custom-call(bf16[6,32,64,128]{3,2,1,0:T(8,128)(2,1)S(1)} %bitcast.10, bf16[3,32,64,128]{3,2,1,0:T(8,128)(2,1)} %collective-permute-done.lo_ref, bf16[3,32,64,128]{3,2,1,0:T(8,128)(2,1)} %collective-permute-done.1.hi_ref, ...), custom_call_target="tpu_custom_call" | custom-call | flops 4000000000 | bytes 30000000 | tf_op jit(solution)/shard_map/stencil/pallas_call | solution.py:175
  69.1 1.7 copy-done.1
  70.8 1.9 %copy-done.2 = bf16[6,32,64,128]{3,2,1,0:T(8,128)(2,1)S(1)} copy-done((bf16[6,32,64,128]{3,2,1,0:T(8,128)(2,1)S(1)}, bf16[6,32,64,128]{3,2,1,0:T(8,128)(2,1)}, u32[]{:S(2)}) %copy-start.2) | copy-done | bytes 3145752
  72.7 5.0 %chip_products.1.v_ref = f32[128,128]{1,0:T(8,128)S(1)} custom-call(bf16[6,32,64,128]{3,2,1,0:T(8,128)(2,1)S(1)} %bitcast.11, bf16[6,32,64,128]{3,2,1,0:T(8,128)(2,1)S(1)} %copy-done.2, bf16[6,32,64,128]{3,2,1,0:T(8,128)(2,1)} %collective-permute-done.2.par_ref), custom_call_target="tpu_custom_call" | custom-call | flops 1000000000 | bytes 9500000 | tf_op jit(solution)/shard_map/chip_products/pallas_call | solution.py:221
  77.7 62.6 %grid_sum.2.refs_3_ = f32[128,128]{1,0:T(8,128)S(1)} custom-call(f32[128,128]{1,0:T(8,128)S(1)} %chip_products.1.v_ref), custom_call_target="tpu_custom_call" | custom-call | tf_op jit(solution)/shard_map/grid_sum/pallas_call | solution.py:94
  140.4 6.1 %cross_products.1.v_ref = f32[128,128]{1,0:T(8,128)S(1)} custom-call(bf16[6,32,64,128]{3,2,1,0:T(8,128)(2,1)S(1)} %bitcast.12, bf16[6,32,64,128]{3,2,1,0:T(8,128)(2,1)} %collective-permute-done.2.par_ref, bf16[6,18,64,128]{3,2,1,0:T(8,128)(2,1)} %get-tuple-element.8.g_ref, bf16[6,18,64,128]{3,2,1,0:T(8,128)(2,1)} %collective-permute-done.3.gpar_ref, ...), custom_call_target="tpu_custom_call" | custom-call | flops 1000000000 | bytes 11000000 | tf_op jit(solution)/shard_map/cross_products/pallas_call | solution.py:272
  146.5 20.2 %grid_sum.3 = f32[128,128]{1,0:T(8,128)S(1)} custom-call(f32[128,128]{1,0:T(8,128)S(1)} %cross_products.1.v_ref), custom_call_target="tpu_custom_call" | custom-call | tf_op jit(solution)/shard_map/grid_sum/pallas_call | solution.py:94
  166.7 0.7 copy.7
  167.5 3.7 %collective-permute-start.5 = (f32[128,128]{0,1:T(8,128)}, f32[128,128]{0,1:T(8,128)S(1)}, u32[]{:S(2)}, u32[]{:S(2)}) collective-permute-start(f32[128,128]{0,1:T(8,128)} %copy.7), channel_id=1, source_target_pairs={{0,128},{64,192},{128,0},{192,64},{1,129},{65,193},{129,1},{193,65... | collective-permute-start | bytes 196616 | tf_op jit(solution)/shard_map/ppermute | solution.py:354
  171.3 2.8 %copy-done = f32[6,32,64,128]{3,2,1,0:T(8,128)S(1)} copy-done((f32[6,32,64,128]{3,2,1,0:T(8,128)S(1)}, f32[6,32,64,128]{3,2,1,0:T(8,128)}, u32[]{:S(2)}) %copy-start) | copy-done | bytes 6291480
  174.0 9.6 %gradient.1 = f32[64,6,32,128]{3,2,1,0:T(8,128)} custom-call(f32[6,32,64,128]{3,2,1,0:T(8,128)S(1)} %copy-done, bf16[6,32,64,128]{3,2,1,0:T(8,128)(2,1)S(1)} %bitcast.13, f32[6,32,128]{2,1,0:T(8,128)S(1)} %copy-done.3, f32[128,128]{1,0:T(8,128)S(1)} %grid_sum.2.refs_3_), custom_call_target="tpu_custom_call" | custom-call | flops 10000000 | bytes 16000000 | tf_op jit(solution)/shard_map/gradient/pallas_call | solution.py:313
  183.7 1.2 collective-permute-done.6
  184.9 0.1 slice_add_fusion.1
  185.0 0.1 maximum_select_fusion.3
  185.1 0.6 fusion.1
  185.8 0.6 fusion
  (16 shorter events, 0.2 us)
Async XLA Ops:
  7.6 36.5 %collective-permute-start = (bf16[3,32,64,128]{3,2,1,0:T(8,128)(2,1)}, bf16[3,32,64,128]{3,2,1,0:T(8,128)(2,1)}, u32[]{:S(2)}, u32[]{:S(2)}) collective-permute-start(bf16[3,32,64,128]{3,2,1,0:T(8,128)(2,1)} %get-tuple-element.12), channel_id=1, source_target_pairs={{0,1},{1,2},{2,3},{3,4},{4,5},{5,6},{6,7},{7,8},{8,9},{9,10},{10,1... | collective-permute-start | bytes 4718600 | tf_op jit(solution)/shard_map/ppermute | solution.py:343
  9.1 36.2 %collective-permute-start.1 = (bf16[3,32,64,128]{3,2,1,0:T(8,128)(2,1)}, bf16[3,32,64,128]{3,2,1,0:T(8,128)(2,1)}, u32[]{:S(2)}, u32[]{:S(2)}) collective-permute-start(bf16[3,32,64,128]{3,2,1,0:T(8,128)(2,1)} %get-tuple-element.11), channel_id=1, source_target_pairs={{1,0},{2,1},{3,2},{4,3},{5,4},{6,5},{7,6},{8,7},{9,8},{10,9},{11,1... | collective-permute-start | bytes 4718600 | tf_op jit(solution)/shard_map/ppermute | solution.py:344
  9.9 60.9 %collective-permute-start.2 = (bf16[6,32,64,128]{3,2,1,0:T(8,128)(2,1)S(1)}, bf16[6,32,64,128]{3,2,1,0:T(8,128)(2,1)}, u32[]{:S(2)}, u32[]{:S(2)}) collective-permute-start(bf16[6,32,64,128]{3,2,1,0:T(8,128)(2,1)S(1)} %bitcast.9), channel_id=1, source_target_pairs={{0,64},{64,0},{128,192},{192,128},{1,65},{65,1},{129,193},{193,129... | collective-permute-start | bytes 9437192 | tf_op jit(solution)/shard_map/ppermute | solution.py:345
  9.9 35.4 %copy-start.3 = (f32[6,32,128]{2,1,0:T(8,128)S(1)}, f32[6,32,128]{2,1,0:T(8,128)}, u32[]{:S(2)}) copy-start(f32[6,32,128]{2,1,0:T(8,128)} %refs_2_.1) | copy-start | bytes 294916
  11.3 129.0 %collective-permute-start.4 = (bf16[6,18,64,128]{3,2,1,0:T(8,128)(2,1)}, bf16[6,18,64,128]{3,2,1,0:T(8,128)(2,1)}, u32[]{:S(2)}, u32[]{:S(2)}) collective-permute-start(bf16[6,18,64,128]{3,2,1,0:T(8,128)(2,1)} %dynamic-slice_bitcast_fusion), channel_id=1, source_target_pairs={{0,128},{64,192},{128,0},{192,64},{1,129},{65,193},{129,1},{193,65... | collective-permute-start | bytes 5308424 | tf_op jit(solution)/shard_map/ppermute | solution.py:342
  69.1 1.7 copy-start.1
  70.8 69.6 %collective-permute-start.3 = (bf16[6,18,64,128]{3,2,1,0:T(8,128)(2,1)}, bf16[6,18,64,128]{3,2,1,0:T(8,128)(2,1)}, u32[]{:S(2)}, u32[]{:S(2)}) collective-permute-start(bf16[6,18,64,128]{3,2,1,0:T(8,128)(2,1)} %get-tuple-element.8.g_ref), channel_id=1, source_target_pairs={{0,64},{64,0},{128,192},{192,128},{1,65},{65,1},{129,193},{193,129... | collective-permute-start | bytes 5308424 | tf_op jit(solution)/shard_map/ppermute | solution.py:348
  70.8 1.9 %copy-start.2 = (bf16[6,32,64,128]{3,2,1,0:T(8,128)(2,1)S(1)}, bf16[6,32,64,128]{3,2,1,0:T(8,128)(2,1)}, u32[]{:S(2)}) copy-start(bf16[6,32,64,128]{3,2,1,0:T(8,128)(2,1)} %copy-done.1) | copy-start | bytes 9437188
  167.5 16.2 %collective-permute-start.5 = (f32[128,128]{0,1:T(8,128)}, f32[128,128]{0,1:T(8,128)S(1)}, u32[]{:S(2)}, u32[]{:S(2)}) collective-permute-start(f32[128,128]{0,1:T(8,128)} %copy.7), channel_id=1, source_target_pairs={{0,128},{64,192},{128,0},{192,64},{1,129},{65,193},{129,1},{193,65... | collective-permute-start | bytes 196616 | tf_op jit(solution)/shard_map/ppermute | solution.py:354
  171.3 2.8 %copy-start = (f32[6,32,64,128]{3,2,1,0:T(8,128)S(1)}, f32[6,32,64,128]{3,2,1,0:T(8,128)}, u32[]{:S(2)}) copy-start(f32[6,32,64,128]{3,2,1,0:T(8,128)} %get-tuple-element.6.refs_0_) | copy-start | bytes 18874372
  183.7 1.2 collective-permute-start.6

commit v3 on v2

v3 whole, which is shorter than its diff:
```python
import jax
import jax.numpy as jnp
from jax import lax
from jax.experimental import pallas as pl
from jax.experimental.pallas import tpu as pltpu
from jax.sharding import PartitionSpec as P

COEFFS = (-49.0 / 18.0, 3.0 / 2.0, -3.0 / 20.0, 1.0 / 90.0)
HALVED = tuple(-0.5 * c for c in COEFFS)
REACH = len(COEFFS) - 1
MESH = pl.DeviceIdType.MESH
F32 = jnp.float32
BF16 = jnp.bfloat16

CUT = 18
WINDOW = 18
EARLY = (4, 3)
FIRST = sum(EARLY)
SMALL = pl.CostEstimate(flops=1000, bytes_accessed=1000, transcendentals=0)


def upper_chip():
    return lax.div(lax.axis_index("band"), 2)


STRIDES = (1, 16, 4)
SIDE = 4


def sum_kernel(cells, near_ref, cross_ref, s_ref, h_ref, chip_ref, b0, bx, by, bz, qx, gy, gx, far, par, send_sem, recv_sem):
    me, band = lax.axis_index("grid"), lax.axis_index("band")
    upper, core = lax.div(band, 2), lax.rem(band, 2)
    rows = near_ref.shape[0]
    rows_x, rows_y = rows // SIDE, rows // SIDE // SIDE
    coord = [lax.rem(lax.div(me, s), SIDE) for s in STRIDES]
    far_band = lax.rem(band + 2, 4)
    par_band = band + 1 - 2 * core

    def peer(axis, d, of=band):
        other = lax.rem(coord[axis] + d, SIDE)
        return other, (of, me + (other - coord[axis]) * STRIDES[axis])

    barrier = pltpu.get_barrier_semaphore()

    def greet(device):
        pl.semaphore_signal(barrier, inc=1, device_id=device, device_id_type=MESH)

    for axis in range(3):
        for d in range(1, SIDE):
            greet(peer(axis, d)[1])
    for of in (far_band, par_band):
        for d in range(SIDE):
            greet(peer(0, d, of)[1])

    def send(phase, d, src, dst, device):
        copy = pltpu.make_async_remote_copy(
            src_ref=src,
            dst_ref=dst,
            send_sem=send_sem.at[phase, d],
            recv_sem=recv_sem.at[phase, d],
            device_id=device,
            device_id_type=MESH,
        )
        copy.start()
        return copy

    def exchange(phase, axis, source, landing):
        copies = []
        for d in range(1, SIDE):
            other, device = peer(axis, d)
            copies.append(send(phase, d, source(other), landing, device))
        return copies

    def finish(copies):
        for copy in copies:
            copy.wait()

    def total(ref):
        return (ref[0] + ref[1]) + (ref[2] + ref[3])

    x, y, z = coord
    for c in range(SIDE):
        b0[c, 0] = near_ref[c * rows_x : (c + 1) * rows_x]
        b0[c, 1] = cross_ref[c * rows_x : (c + 1) * rows_x]
    pl.semaphore_wait(barrier, 3 * (SIDE - 1) + 2 * SIDE)

    copies = exchange(0, 0, lambda c: b0.at[c], bx.at[x])
    bx[x] = b0[x]
    finish(copies)
    summed = total(bx)
    for c in range(SIDE):
        qx[c] = summed[:, c * rows_y : (c + 1) * rows_y]

    copies = exchange(1, 1, lambda c: qx.at[c], by.at[y])
    by[y] = qx[y]
    finish(copies)
    bz[z] = total(by)

    finish(exchange(2, 2, lambda c: bz.at[z], bz.at[z]))
    gy[y] = total(bz)

    finish(exchange(3, 1, lambda c: gy.at[y], gy.at[y]))
    for c in range(SIDE):
        gx[x, :, c * rows_y : (c + 1) * rows_y] = gy[c]

    copies = exchange(4, 0, lambda c: gx.at[x], gx.at[x])
    for d in range(SIDE):
        copies.append(send(5, d, gx.at[x, 1], far.at[x], peer(0, d, far_band)[1]))
        copies.append(send(6, d, gx.at[x, 1], par.at[x], peer(0, d, par_band)[1]))
    finish(copies)

    def whole(ref, i=None):
        return jnp.concatenate([ref[c] if i is None else ref[c, i] for c in range(SIDE)], axis=0)

    chip, cross = whole(gx, 0), whole(gx, 1)
    chip_ref[...] = chip
    orbs = rows // 2
    par_rows = jnp.concatenate([par[c] for c in range(SIDE // 2, SIDE)], axis=0)
    turned = whole(far).T
    for which, o_ref in ((0, s_ref), (1, h_ref)):
        columns = slice(which * orbs, (which + 1) * orbs)
        mine = chip[which * orbs : (which + 1) * orbs]
        away = turned[columns] + jnp.concatenate([cross[:orbs, columns], par_rows[:, columns]], axis=1)
        mine = jnp.where(core == 0, mine, pltpu.roll(mine, orbs, 1)) / cells
        away = jnp.where(core == 0, away, pltpu.roll(away, orbs, 1)) / cells
        o_ref[:, :rows] = jnp.where(upper == 0, mine, away)
        o_ref[:, rows:] = jnp.where(upper == 0, away, mine)


def sums_of(near, cross, cells, collective_id):
    rows, cols = near.shape
    rows_x, rows_y = rows // SIDE, rows // SIDE // SIDE
    vmem = pl.BlockSpec(memory_space=pltpu.VMEM)
    wide = pltpu.VMEM((SIDE, 2, rows_x, cols), F32)
    slim = pltpu.VMEM((SIDE, 2, rows_y, cols), F32)
    part = pltpu.VMEM((SIDE, rows_x, cols), F32)
    out = jax.ShapeDtypeStruct((rows // 2, 2 * rows), F32)
    return pl.pallas_call(
        lambda *refs: sum_kernel(cells, *refs),
        out_shape=(out, out, jax.ShapeDtypeStruct((rows, cols), F32)),
        in_specs=[vmem, vmem],
        out_specs=(vmem, vmem, vmem),
        scratch_shapes=[wide, wide, slim, slim, slim, slim, wide, part, part]
        + [pltpu.SemaphoreType.DMA((7, SIDE))] * 2,
        compiler_params=pltpu.CompilerParams(
            collective_id=collective_id, has_side_effects=True, vmem_limit_bytes=6 << 20
        ),
        name="grid_sums",
    )(near, cross)


def halo_kernel(psi_ref, lo_ref, hi_ref, far_ref, up_a, up_b, down_a, down_b, send_sem, recv_sem):
    me, band = lax.axis_index("grid"), lax.axis_index("band")
    x, row = lax.rem(me, SIDE), lax.div(me, SIDE)
    rows = SIDE * SIDE
    after, before = lax.rem(row + 1, rows), lax.rem(row + rows - 1, rows)
    layers, planes = psi_ref.shape[:2]
    share = planes // SIDE
    last = SIDE - 1

    def device(column, line):
        return (band, line * SIDE + column)

    barrier = pltpu.get_barrier_semaphore()
    for d in range(1, SIDE):
        pl.semaphore_signal(
            barrier, inc=1, device_id=device(lax.rem(x + d, SIDE), row), device_id_type=MESH
        )
    for line in (after, before):
        pl.semaphore_signal(barrier, inc=1, device_id=device(x, line), device_id_type=MESH)
    twin = (lax.rem(band + 2, 4), me)
    pl.semaphore_signal(barrier, inc=1, device_id=twin, device_id_type=MESH)
    pl.semaphore_wait(barrier, SIDE + 2)

    tail = psi_ref.at[pl.ds(layers - REACH, REACH)]
    head = psi_ref.at[pl.ds(0, REACH)]

    def piece(ref, q):
        start = q * share
        return ref.at[:, pl.ds(start if isinstance(q, int) else pl.multiple_of(start, share), share)]

    def copy(src, dst, sent, received, target):
        return pltpu.make_async_remote_copy(
            src_ref=src,
            dst_ref=dst,
            send_sem=send_sem.at[sent],
            recv_sem=recv_sem.at[received],
            device_id=target,
            device_id_type=MESH,
        )

    LO, HI, UP_A, UP_B, DOWN_A, DOWN_B, LO_PART, HI_PART = 0, 1, 2, 3, 4, 5, 6, 6 + SIDE
    FAR = 6 + 2 * SIDE
    own = device(x, row)
    wanted = (1 - upper_chip()) * (planes - WINDOW)

    def far_copy(i):
        begin = sum(EARLY[:i])
        return copy(
            psi_ref.at[:, pl.ds(wanted + begin, EARLY[i])],
            far_ref.at[:, pl.ds(begin, EARLY[i])],
            10 + i,
            FAR + i,
            twin,
        )

    @pl.when(x == last)
    def _():
        for q in range(last):
            copy(piece(tail, q), up_a, q, UP_A, device(q, row)).start()
        copy(piece(tail, last), up_b, 6, UP_B, device(x, after)).start()

    @pl.when(x == 0)
    def _():
        for q in range(1, SIDE):
            copy(piece(head, q), down_a, q, DOWN_A, device(q, row)).start()
        copy(piece(head, 0), down_b, 7, DOWN_B, device(x, before)).start()

    @pl.when(x < last)
    def _():
        copy(tail, lo_ref, 4, LO, device(x + 1, row)).start()

    @pl.when(x > 0)
    def _():
        copy(head, hi_ref, 5, HI, device(x - 1, row)).start()

    far_copy(0).start()

    @pl.when(x < last)
    def _():
        copy(piece(tail, 0), up_a, 0, UP_A, own).wait_recv()

    @pl.when(x == 0)
    def _():
        copy(up_a, piece(lo_ref, 0), 6, LO_PART, device(x, after)).start()

    @pl.when((x > 0) & (x < last))
    def _():
        copy(up_a, up_b, 6, UP_B, device(x, after)).start()

    @pl.when(x > 0)
    def _():
        copy(piece(head, 0), down_a, 0, DOWN_A, own).wait_recv()

    @pl.when(x == last)
    def _():
        copy(down_a, piece(hi_ref, last), 7, HI_PART + last, device(x, before)).start()

    @pl.when((x > 0) & (x < last))
    def _():
        copy(down_a, down_b, 7, DOWN_B, device(x, before)).start()

    far_copy(1).start()

    @pl.when(x > 0)
    def _():
        copy(up_a, up_b, 6, UP_B, own).wait_recv()
        copy(up_b, piece(lo_ref, x), 8, LO_PART + x, device(0, row)).start()

    @pl.when(x < last)
    def _():
        copy(down_a, down_b, 7, DOWN_B, own).wait_recv()
        copy(down_b, piece(hi_ref, x), 9, HI_PART + x, device(last, row)).start()

    @pl.when(x == 0)
    def _():
        for q in range(SIDE):
            copy(up_b, piece(lo_ref, q), 8, LO_PART + q, own).wait_recv()
        for q in range(1, SIDE):
            copy(piece(head, q), down_a, q, DOWN_A, own).wait_send()

    @pl.when(x == last)
    def _():
        for q in range(SIDE):
            copy(down_b, piece(hi_ref, q), 9, HI_PART + q, own).wait_recv()
        for q in range(last):
            copy(piece(tail, q), up_a, q, UP_A, own).wait_send()

    @pl.when(x > 0)
    def _():
        copy(tail, lo_ref, 4, LO, own).wait_recv()
        copy(head, hi_ref, 5, HI, own).wait_send()
        copy(up_b, piece(lo_ref, 0), 8, LO_PART, own).wait_send()

    @pl.when(x < last)
    def _():
        copy(head, hi_ref, 5, HI, own).wait_recv()
        copy(tail, lo_ref, 4, LO, own).wait_send()
        copy(down_b, piece(hi_ref, 0), 9, HI_PART, own).wait_send()

    copy(up_a, up_b, 6, UP_B, own).wait_send()
    copy(down_a, down_b, 7, DOWN_B, own).wait_send()
    for i in range(len(EARLY)):
        far_copy(i).wait()


def halo(psi, collective_id):
    layers, planes, orbs, ny = psi.shape
    edge = jax.ShapeDtypeStruct((REACH, planes, orbs, ny), psi.dtype)
    part = pltpu.VMEM((REACH, planes // SIDE, orbs, ny), psi.dtype)
    return pl.pallas_call(
        halo_kernel,
        out_shape=(edge, edge, jax.ShapeDtypeStruct((layers, FIRST, orbs, ny), psi.dtype)),
        in_specs=[pl.BlockSpec(memory_space=pl.ANY)],
        out_specs=(pl.BlockSpec(memory_space=pl.ANY),) * 3,
        scratch_shapes=[
            part,
            part,
            part,
            part,
            pltpu.SemaphoreType.DMA((12,)),
            pltpu.SemaphoreType.DMA((8 + 2 * SIDE,)),
        ],
        compiler_params=pltpu.CompilerParams(
            collective_id=collective_id, has_side_effects=True, vmem_limit_bytes=8 << 20
        ),
        cost_estimate=SMALL,
        name="halo",
    )(psi)


def stencil_kernel(psi_ref, lo_ref, hi_ref, v_ref, hpsi_ref, half_ref, g_ref, field):
    layers, planes = psi_ref.shape[:2]

    @pl.when(pl.program_id(0) == 0)
    def _():
        edge = jnp.zeros((layers + 2 * REACH, REACH) + psi_ref.shape[2:], F32)
        field[:, :REACH] = edge
        field[:, REACH + planes :] = edge

    @pl.loop(0, planes, unroll=4)
    def _(z):
        for x in range(REACH):
            field[x, z + REACH] = lo_ref[x, z].astype(F32)
            field[x + REACH + layers, z + REACH] = hi_ref[x, z].astype(F32)
        for x in range(layers):
            field[x + REACH, z + REACH] = psi_ref[x, z].astype(F32)

    @pl.loop(0, planes, unroll=4)
    def _(z):
        for x in range(layers):
            i, j = x + REACH, z + REACH
            center = field[i, j]
            total = (3.0 * HALVED[0] + v_ref[x, pl.ds(z, 1), :]) * center
            for k in range(1, REACH + 1):
                pair_x = field[i + k, j] + field[i - k, j]
                pair_z = field[i, j + k] + field[i, j - k]
                pair_y = pltpu.roll(center, k, 1) + pltpu.roll(center, center.shape[1] - k, 1)
                total = total + HALVED[k] * (pair_x + pair_z + pair_y)
            hpsi_ref[x, z] = total
            half_ref[x, z] = total.astype(BF16)

    upper = upper_chip()
    first = upper * (planes - WINDOW)

    @pl.loop(0, WINDOW, unroll=2)
    def _(i):
        for x in range(layers):
            g_ref[x, i] = half_ref[x, first + i]

    @pl.when(upper == 1)
    def _():
        for x in range(layers):
            for z in range(planes - WINDOW, CUT + REACH):
                if z < CUT:
                    total = jnp.zeros(psi_ref.shape[2:], F32)
                    for k in range(CUT - z, REACH + 1):
                        total = total + HALVED[k] * field[x + REACH, z + REACH + k]
                else:
                    total = hpsi_ref[x, z]
                    for k in range(z - CUT + 1, REACH + 1):
                        total = total - HALVED[k] * field[x + REACH, z + REACH - k]
                g_ref[x, z - (planes - WINDOW)] = total.astype(BF16)


def stencil(psi, lo, hi, potential):
    layers, planes, orbs, ny = psi.shape
    block = 16

    def spec(n, m):
        return pl.BlockSpec((n, m, block, ny), lambda o: (0, 0, o, 0))

    return pl.pallas_call(
        stencil_kernel,
        grid=(orbs // block,),
        out_shape=(
            jax.ShapeDtypeStruct(psi.shape, F32),
            jax.ShapeDtypeStruct(psi.shape, BF16),
            jax.ShapeDtypeStruct((layers, WINDOW, orbs, ny), BF16),
        ),
        in_specs=[
            spec(layers, planes),
            spec(REACH, planes),
            spec(REACH, planes),
            pl.BlockSpec(potential.shape, lambda o: (0, 0, 0)),
        ],
        out_specs=(spec(layers, planes), spec(layers, planes), spec(layers, WINDOW)),
        scratch_shapes=[pltpu.VMEM((layers + 2 * REACH, planes + 2 * REACH, block, ny), F32)],
        compiler_params=pltpu.CompilerParams(vmem_limit_bytes=40 << 20),
        cost_estimate=SMALL,
        name="stencil",
    )(psi, lo, hi, potential)


def partner_kernel(src_ref, dst_ref, send_sem, recv_sem):
    band, me = lax.axis_index("band"), lax.axis_index("grid")
    partner = (band + 1 - 2 * lax.rem(band, 2), me)
    barrier = pltpu.get_barrier_semaphore()
    pl.semaphore_signal(barrier, inc=1, device_id=partner, device_id_type=MESH)
    pl.semaphore_wait(barrier, 1)
    copy = pltpu.make_async_remote_copy(
        src_ref=src_ref,
        dst_ref=dst_ref,
        send_sem=send_sem,
        recv_sem=recv_sem,
        device_id=partner,
        device_id_type=MESH,
    )
    copy.start()
    copy.wait()


def from_partner(array, collective_id):
    return pl.pallas_call(
        partner_kernel,
        out_shape=jax.ShapeDtypeStruct(array.shape, array.dtype),
        in_specs=[pl.BlockSpec(memory_space=pl.ANY)],
        out_specs=pl.BlockSpec(memory_space=pl.ANY),
        scratch_shapes=[pltpu.SemaphoreType.DMA, pltpu.SemaphoreType.DMA],
        compiler_params=pltpu.CompilerParams(
            collective_id=collective_id, has_side_effects=True, vmem_limit_bytes=1 << 20
        ),
        cost_estimate=SMALL,
        name="from_partner",
    )(array)


def contract(left, right):
    return lax.dot_general(left, right, (((1,), (1,)), ((), ())), preferred_element_type=F32)


def chip_kernel(psi_ref, half_ref, par_ref, o_ref):
    @pl.when(pl.program_id(0) == 0)
    def _():
        o_ref[...] = jnp.zeros_like(o_ref)

    planes = psi_ref.shape[1]
    group = 8
    for z in range(0, planes, group):
        def wide(ref):
            return jnp.concatenate([ref[0, z + i] for i in range(group)], axis=1)

        psi = wide(psi_ref)
        left = jnp.concatenate([psi, wide(half_ref)], axis=0)
        right = jnp.concatenate([psi, wide(par_ref)], axis=0)
        o_ref[...] += contract(left, right)


def chip_products(psi, half, par):
    layers, planes, orbs, ny = psi.shape
    spec = pl.BlockSpec((1, planes, orbs, ny), lambda x: (x, 0, 0, 0))
    return pl.pallas_call(
        chip_kernel,
        grid=(layers,),
        out_shape=jax.ShapeDtypeStruct((2 * orbs, 2 * orbs), F32),
        in_specs=[spec, spec, spec],
        out_specs=pl.BlockSpec((2 * orbs, 2 * orbs), lambda x: (0, 0)),
        compiler_params=pltpu.CompilerParams(vmem_limit_bytes=24 << 20),
        cost_estimate=SMALL,
        name="chip_products",
    )(psi, half, par)


def cross_kernel(begin, psi_ref, par_ref, g_ref, gpar_ref, far_ref, *rest):
    acc = rest[-1]

    @pl.when(pl.program_id(0) == 0)
    def _():
        acc[...] = jnp.zeros_like(acc) if begin == 0 else rest[0][...]

    planes, count = psi_ref.shape[1], far_ref.shape[1]
    upper = upper_chip()
    first = upper * (planes - WINDOW)
    keep = (1 - upper).astype(F32).astype(BF16)
    skipped = CUT - (planes - WINDOW)
    group = 4
    for z in range(0, count, group):
        mine = range(z, min(z + group, count))

        def wide(ref, offset, masked=False):
            parts = [ref[0, offset + i] for i in mine]
            if masked:
                parts = [p * keep if begin + i < skipped else p for i, p in zip(mine, parts)]
            return jnp.concatenate(parts, axis=1)

        left = jnp.concatenate(
            [
                wide(psi_ref, first + begin, True),
                wide(par_ref, first + begin, True),
                wide(g_ref, begin),
                wide(gpar_ref, begin),
            ],
            axis=0,
        )
        acc[...] += contract(left, wide(far_ref, 0))

    if begin:
        o_ref = rest[1]

        @pl.when(pl.program_id(0) == pl.num_programs(0) - 1)
        def _():
            rows = acc.shape[0] // 2
            o_ref[...] = jnp.concatenate([acc[:rows], acc[rows:]], axis=1)


def cross_products(psi, par, g, g_par, far, begun=None):
    layers, planes, orbs, ny = psi.shape
    begin = 0 if begun is None else FIRST

    def spec(n):
        return pl.BlockSpec((1, n, orbs, ny), lambda x: (x, 0, 0, 0))

    def fixed(shape):
        return pl.BlockSpec(shape, lambda x: (0, 0))

    tall, square = (4 * orbs, orbs), (2 * orbs, 2 * orbs)
    shape = square if begin else tall
    return pl.pallas_call(
        lambda *refs: cross_kernel(begin, *refs),
        grid=(layers,),
        out_shape=jax.ShapeDtypeStruct(shape, F32),
        in_specs=[spec(planes), spec(planes), spec(WINDOW), spec(WINDOW), spec(far.shape[1])]
        + ([fixed(tall)] if begin else []),
        out_specs=fixed(shape),
        scratch_shapes=[pltpu.VMEM(tall, F32)] if begin else [],
        compiler_params=pltpu.CompilerParams(vmem_limit_bytes=24 << 20),
        cost_estimate=SMALL,
        name="cross_products_%d" % begin,
    )(psi, par, g, g_par, far, *([begun] if begin else []))


def turn_kernel(hpsi_ref, v_ref, o_ref):
    v = v_ref[0]
    parts = [hpsi_ref[0, z] / (2.0 + v[z : z + 1]) for z in range(hpsi_ref.shape[1])]
    o_ref[:, 0] = jnp.swapaxes(jnp.stack(parts, axis=0), 0, 1)


def turn(hpsi, potential):
    layers, planes, orbs, ny = hpsi.shape
    block = 8
    return pl.pallas_call(
        turn_kernel,
        grid=(layers, planes // block),
        out_shape=jax.ShapeDtypeStruct((orbs, layers, planes, ny), F32),
        in_specs=[
            pl.BlockSpec((1, block, orbs, ny), lambda x, z: (x, z, 0, 0)),
            pl.BlockSpec((1, block, ny), lambda x, z: (x, z, 0)),
        ],
        out_specs=pl.BlockSpec((orbs, 1, block, ny), lambda x, z: (0, x, z, 0)),
        compiler_params=pltpu.CompilerParams(vmem_limit_bytes=16 << 20),
        cost_estimate=SMALL,
        name="turn",
    )(hpsi, potential)


def gradient_kernel(cells, part_ref, psi_ref, v_ref, sums_ref, o_ref, ray, weight):
    orbs = ray.shape[0]
    block = o_ref.shape[0]

    @pl.when(pl.program_id(0) == 0)
    def _():
        shape = (orbs, orbs)
        same = lax.broadcasted_iota(jnp.int32, shape, 0) == lax.broadcasted_iota(jnp.int32, shape, 1)

        def diagonal(rows):
            picked = jnp.where(same, sums_ref[rows : rows + orbs, :orbs], 0.0)
            return jnp.sum(picked, axis=1, keepdims=True) / cells

        ray[...] = jnp.broadcast_to(diagonal(orbs) / (diagonal(0) + 1e-06), ray.shape)
        weight[...] = 1.0 / (2.0 + v_ref[...])

    for i in range(block):
        rayleigh = ray[pl.ds(pl.program_id(0) * block + i, 1), :]
        for x in range(o_ref.shape[1]):
            o_ref[i, x] = part_ref[i, x] - (rayleigh * weight[x]) * psi_ref[i, x].astype(F32)


def gradient_of(part, orbitals, potential, sums, cells):
    orbs, layers, planes, ny = orbitals.shape
    block = 8
    spec = pl.BlockSpec((block, layers, planes, ny), lambda o: (o, 0, 0, 0))
    return pl.pallas_call(
        lambda *refs: gradient_kernel(cells, *refs),
        grid=(orbs // block,),
        out_shape=jax.ShapeDtypeStruct(orbitals.shape, F32),
        in_specs=[
            spec,
            spec,
            pl.BlockSpec(potential.shape, lambda o: (0, 0, 0)),
            pl.BlockSpec(sums.shape, lambda o: (0, 0)),
        ],
        out_specs=spec,
        scratch_shapes=[pltpu.VMEM((orbs, ny), F32), pltpu.VMEM(potential.shape, F32)],
        compiler_params=pltpu.CompilerParams(vmem_limit_bytes=16 << 20),
        name="gradient",
    )(part, orbitals, potential, sums)


def body(orbitals, potential):
    orbs, layers, planes, ny = orbitals.shape
    cells = layers * lax.axis_size("grid") * planes * ny
    upper = upper_chip()
    other_core = [(0, 1), (1, 0), (2, 3), (3, 2)]
    other_chip = [(0, 2), (1, 3), (2, 0), (3, 1)]

    psi = jnp.transpose(orbitals, (1, 2, 0, 3))
    par = lax.ppermute(psi, "band", other_core)
    lo, hi, far_first = halo(psi, 3)
    begin = (1 - upper) * (planes - WINDOW) + FIRST
    wanted = lax.dynamic_slice_in_dim(psi, begin, WINDOW - FIRST, 1)
    wanted, far_first, lo = lax.optimization_barrier((wanted, far_first, lo))
    far = lax.ppermute(wanted, "band", other_chip)

    hpsi, half, g = stencil(psi, lo, hi, potential)
    g_par = from_partner(g, 2)
    near = chip_products(psi, half, par)
    part = turn(hpsi, potential)
    begun = cross_products(psi, par, g, g_par, far_first)
    far, part, near, begun = lax.optimization_barrier((far, part, near, begun))
    cross = cross_products(psi, par, g, g_par, far, begun)
    intersection, subspace, chip = sums_of(near, cross, cells, 1)
    gradient = gradient_of(part, orbitals, potential, chip, cells)
    return (gradient, intersection, subspace)


def solution(mesh):
    in_specs = (P("band", "grid", None, None), P("grid", None, None))
    out_specs = (P("band", "grid", None, None), P("band", None), P("band", None))
    return jax.shard_map(body, mesh=mesh, in_specs=in_specs, out_specs=out_specs, check_vma=False)
```

time: 189 us -> 160 us (0.85)
  waiting for transfers between devices: 28.2 us -> 12.5 us
  starting transfers between devices: 12.9 us -> 4.56 us
  local copies, waits for them, and re-layouts: 15.6 us -> 12.6 us
    ppermute x5 -> x0, waiting for transfers between devices: 28.2 us -> none  [the longest x1 25.8 us: body(): lax.ppermute(psi[layers - REACH:], 'grid', [(i, (i + 1) % grids) for i in...]
    ppermute x1, waiting for transfers between devices: 0.01 us -> 12.5 us  [body(): far = lax.ppermute(wanted, 'band', other_chip)]
    pallas_call x4 -> x7, Pallas kernels: 98.6 us -> 107 us  [the longest x1 59.7 us: halo(): pl.pallas_call(halo_kernel, out_shape=(edge, edge, jax.ShapeDtypeStruct((...]
    pallas_call x1, Pallas kernels: 23.8 us -> 15.9 us  [stencil(): pl.pallas_call(stencil_kernel, grid=(orbs // block,), out_shape=(jax.Shap...]
    ppermute x5 -> x0, starting transfers between devices: 5.95 us -> none  [the longest x1 3.7 us: body(): cross_far = lax.ppermute(cross, 'band', other_chip)]
    slice x3 -> x0, local copies, waits for them, and re-layouts: 3.17 us -> none  [the longest x1 3.09 us: body(): psi[:REACH]]
    ppermute x1, starting transfers between devices: 6.97 us -> 4.46 us  [body(): far = lax.ppermute(wanted, 'band', other_chip)]
    unnamed x9 -> x21, local copies, waits for them, and re-layouts: 10.3 us -> 12.5 us
  transfers between devices with their start and end apart: 7 -> 2, of which waited for: 3 -> 1; matrix products, arithmetic and copies ran while one was open for 1% -> 0% of each run, Pallas kernels for 54% -> 58%
where the time goes in v3:
time: 160 us; the launch traced here: 158 us
  Pallas kernels  128 us (80%)
  local copies, waits for them, and re-layouts  12.6 us (8%)
  waiting for transfers between devices  12.5 us (8%)
  starting transfers between devices  4.56 us (3%)
    pallas_call x1, Pallas kernels, halo(): pl.pallas_call(halo_kernel, out_shape=(edge, edge, jax.ShapeDtypeStruct((...  59.7 us
    pallas_call x1, Pallas kernels, sums_of(): pl.pallas_call(lambda *refs: sum_kernel(cells, *refs), out_shape=(out, ou...  27.6 us
    pallas_call x1, Pallas kernels, stencil(): pl.pallas_call(stencil_kernel, grid=(orbs // block,), out_shape=(jax.Shap...  15.9 us
    unnamed x21, local copies, waits for them, and re-layouts  12.5 us
    ppermute x1, waiting for transfers between devices, body(): far = lax.ppermute(wanted, 'band', other_chip)  12.5 us
    pallas_call x2, Pallas kernels, cross_products(): pl.pallas_call(lambda *refs: cross_kernel(begin, *refs), grid=(layers,),...  9.01 us
    pallas_call x1, Pallas kernels, chip_products(): pl.pallas_call(chip_kernel, grid=(layers,), out_shape=jax.ShapeDtypeStruc...  5.07 us
    ppermute x1, starting transfers between devices, body(): far = lax.ppermute(wanted, 'band', other_chip)  4.46 us
  transfers between devices with their start and end apart: 2, of which 1 were waited for; matrix products, arithmetic and copies ran while one was open for 0% of the time, Pallas kernels for 58%

profile of v3, /device:TPU:2, one launch (start us, length us, event | category | flops | bytes accessed | tf_op | source)
XLA Modules:
  0.0 158.2 jit_solution(2880076356991332891)
XLA Ops:
  0.6 3.9 %copy.9 = bf16[64,6,32,128]{3,0,2,1:T(8,128)(2,1)S(1)} copy(bf16[64,6,32,128]{3,2,1,0:T(8,128)(2,1)} %refs_1_.1) | data formatting | bytes 6291456 | tf_op args[0]
  4.5 0.0 copy-start.6
  4.6 0.1 collective-permute-start.1
  4.7 59.7 %halo.1 = (bf16[3,32,64,128]{3,2,1,0:T(8,128)(2,1)S(1)}, bf16[3,32,64,128]{3,2,1,0:T(8,128)(2,1)S(1)}, bf16[6,7,64,128]{3,2,1,0:T(8,128)(2,1)S(1)}) custom-call(bf16[6,32,64,128]{3,2,1,0:T(8,128)(2,1)S(1)} %bitcast.6), custom_call_target="tpu_custom_call" | custom-call | flops 1000 | bytes 1000 | tf_op jit(solution)/shard_map/halo/pallas_call | solution.py:301
  64.3 0.0 copy-start.2
  64.3 1.1 copy-done.2
  65.5 1.2 copy-done.4
  66.6 0.9 copy-done.7
  67.5 0.1 dynamic-slice_bitcast_fusion
  67.6 4.5 %collective-permute-start = (bf16[6,11,64,128]{3,2,1,0:T(8,128)(2,1)S(1)}, bf16[6,11,64,128]{3,2,1,0:T(8,128)(2,1)S(1)}, u32[]{:S(2)}, u32[]{:S(2)}) collective-permute-start(bf16[6,11,64,128]{3,2,1,0:T(8,128)(2,1)S(1)} %dynamic-slice_bitcast_fusion), channel_id=1, source_target_pairs={{0,128},{64,192},{128,0},{192,64},{1,129},{65,193},{129,1},{193,65... | collective-permute-start | bytes 3244040 | tf_op jit(solution)/shard_map/ppermute | solution.py:622
  72.1 1.4 copy-done.5
  73.5 15.9 %stencil.1 = (f32[6,32,64,128]{3,2,1,0:T(8,128)}, bf16[6,32,64,128]{3,2,1,0:T(8,128)(2,1)S(1)}, bf16[6,18,64,128]{3,2,1,0:T(8,128)(2,1)S(1)}) custom-call(bf16[6,32,64,128]{3,2,1,0:T(8,128)(2,1)S(1)} %bitcast.7, bf16[3,32,64,128]{3,2,1,0:T(8,128)(2,1)S(1)} %copy-done.3, bf16[3,32,64,128]{3,2,1,0:T(8,128)(2,1)S(1)} %copy-done.5, f32[6,32,128]{2,1,0:T(8,128)S(1)} %copy-done.6), custom_call_target="tpu_custom_call" | custom-call | flops 1000 | bytes 1000 | tf_op jit(solution)/shard_map/stencil/pallas_call | solution.py:383
  89.4 2.8 %copy-done.1 = f32[6,32,64,128]{3,2,1,0:T(8,128)S(1)} copy-done((f32[6,32,64,128]{3,2,1,0:T(8,128)S(1)}, f32[6,32,64,128]{3,2,1,0:T(8,128)}, u32[]{:S(2)}) %copy-start.1) | copy-done | bytes 6291480
  92.2 2.4 %turn.1.refs_0_ = f32[64,6,32,128]{3,2,1,0:T(8,128)S(1)} custom-call(f32[6,32,64,128]{3,2,1,0:T(8,128)S(1)} %copy-done.1, f32[6,32,128]{2,1,0:T(8,128)S(1)} %copy-done.6), custom_call_target="tpu_custom_call" | custom-call | flops 1000 | bytes 1000 | tf_op jit(solution)/shard_map/turn/pallas_call | solution.py:551
  94.5 3.9 %from_partner.1.refs_3_ = bf16[6,18,64,128]{3,2,1,0:T(8,128)(2,1)S(1)} custom-call(bf16[6,18,64,128]{3,2,1,0:T(8,128)(2,1)S(1)} %get-tuple-element.26.src_ref.refs_2_), custom_call_target="tpu_custom_call" | custom-call | flops 1000 | bytes 1000 | tf_op jit(solution)/shard_map/from_partner/pallas_call | solution.py:424
  98.4 5.1 %chip_products.1.refs_0_ = f32[128,128]{1,0:T(8,128)S(1)} custom-call(bf16[6,32,64,128]{3,2,1,0:T(8,128)(2,1)S(1)} %bitcast.8, bf16[6,32,64,128]{3,2,1,0:T(8,128)(2,1)S(1)} %get-tuple-element.25.half_ref, bf16[6,32,64,128]{3,2,1,0:T(8,128)(2,1)} %collective-permute-done.1.par_ref.refs_1_), custom_call_target="tpu_custom_call" | custom-call | flops 1000 | bytes 1000 | tf_op jit(solution)/shard_map/chip_products/pallas_call | solution.py:462
  103.5 4.3 %cross_products_0.1.refs_5_ = f32[256,64]{1,0:T(8,128)S(1)} custom-call(bf16[6,32,64,128]{3,2,1,0:T(8,128)(2,1)S(1)} %bitcast.9, bf16[6,32,64,128]{3,2,1,0:T(8,128)(2,1)} %collective-permute-done.1.par_ref.refs_1_, bf16[6,18,64,128]{3,2,1,0:T(8,128)(2,1)S(1)} %get-tuple-element.26.src_ref.refs_2_, bf16[6,18,64,128]{3,2,1,0:T(8,128)(2,1)S(1)} %from_partner.1.refs_3_, ...), custom_call_target="tpu_custom_call" | custom-call | flops 1000 | bytes 1000 | tf_op jit(solution)/shard_map/cross_products_0/pallas_call | solution.py:528
  107.8 0.0 copy-start
  107.9 12.5 %collective-permute-done.refs_4_ = bf16[6,11,64,128]{3,2,1,0:T(8,128)(2,1)S(1)} collective-permute-done((bf16[6,11,64,128]{3,2,1,0:T(8,128)(2,1)S(1)}, bf16[6,11,64,128]{3,2,1,0:T(8,128)(2,1)S(1)}, u32[]{:S(2)}, u32[]{:S(2)}) %collective-permute-start) | collective-permute-done | bytes 1081376 | tf_op jit(solution)/shard_map/ppermute | solution.py:622
  120.3 4.7 %cross_products_7.1.refs_1_ = f32[128,128]{1,0:T(8,128)S(1)} custom-call(bf16[6,32,64,128]{3,2,1,0:T(8,128)(2,1)S(1)} %bitcast.10, bf16[6,32,64,128]{3,2,1,0:T(8,128)(2,1)} %collective-permute-done.1.par_ref.refs_1_, bf16[6,18,64,128]{3,2,1,0:T(8,128)(2,1)S(1)} %get-tuple-element.26.src_ref.refs_2_, bf16[6,18,64,128]{3,2,1,0:T(8,128)(2,1)S(1)} %from_partner.1.refs_3_, ...), custom_call_target="tpu_custom_call" | custom-call | flops 1000 | bytes 1000 | tf_op jit(solution)/shard_map/cross_products_7/pallas_call | solution.py:528
  125.0 27.6 %grid_sums.1 = (f32[64,256]{1,0:T(8,128)S(1)}, f32[64,256]{1,0:T(8,128)S(1)}, f32[128,128]{1,0:T(8,128)S(1)}) custom-call(f32[128,128]{1,0:T(8,128)S(1)} %chip_products.1.refs_0_, f32[128,128]{1,0:T(8,128)S(1)} %cross_products_7.1.refs_1_), custom_call_target="tpu_custom_call" | custom-call | tf_op jit(solution)/shard_map/grid_sums/pallas_call | solution.py:138
  152.6 4.3 %gradient.1 = f32[64,6,32,128]{3,2,1,0:T(8,128)} custom-call(f32[64,6,32,128]{3,2,1,0:T(8,128)S(1)} %turn.1.refs_0_, bf16[64,6,32,128]{3,2,1,0:T(8,128)(2,1)S(1)} %copy-done, f32[6,32,128]{2,1,0:T(8,128)S(1)} %copy-done.6, f32[128,128]{1,0:T(8,128)S(1)} %get-tuple-element.32.refs_3_), custom_call_target="tpu_custom_call" | custom-call | tf_op jit(solution)/shard_map/gradient/pallas_call | solution.py:592
  157.0 0.6 copy.12
  157.6 0.6 copy.13
  (11 shorter events, 0.0 us)
Async XLA Ops:
  4.5 67.5 %copy-start.6 = (f32[6,32,128]{2,1,0:T(8,128)S(1)}, f32[6,32,128]{2,1,0:T(8,128)}, u32[]{:S(2)}) copy-start(f32[6,32,128]{2,1,0:T(8,128)} %refs_2_.1) | copy-start | bytes 294916
  4.6 93.9 %collective-permute-start.1 = (bf16[6,32,64,128]{3,2,1,0:T(8,128)(2,1)S(1)}, bf16[6,32,64,128]{3,2,1,0:T(8,128)(2,1)}, u32[]{:S(2)}, u32[]{:S(2)}) collective-permute-start(bf16[6,32,64,128]{3,2,1,0:T(8,128)(2,1)S(1)} %bitcast.5), channel_id=1, source_target_pairs={{0,64},{64,0},{128,192},{192,128},{1,65},{65,1},{129,193},{193,129... | collective-permute-start | bytes 9437192 | tf_op jit(solution)/shard_map/ppermute | solution.py:617
  64.3 1.1 copy-start.2
  65.5 1.2 copy-start.4
  66.6 0.9 copy-start.7
  67.5 4.6 %copy-start.3 = (bf16[3,32,64,128]{3,2,1,0:T(8,128)(2,1)S(1)}, bf16[3,32,64,128]{3,2,1,0:T(8,128)(2,1)}, u32[]{:S(2)}) copy-start(bf16[3,32,64,128]{3,2,1,0:T(8,128)(2,1)} %copy-done.2) | copy-start | bytes 4718596
  67.6 52.7 %collective-permute-start = (bf16[6,11,64,128]{3,2,1,0:T(8,128)(2,1)S(1)}, bf16[6,11,64,128]{3,2,1,0:T(8,128)(2,1)S(1)}, u32[]{:S(2)}, u32[]{:S(2)}) collective-permute-start(bf16[6,11,64,128]{3,2,1,0:T(8,128)(2,1)S(1)} %dynamic-slice_bitcast_fusion), channel_id=1, source_target_pairs={{0,128},{64,192},{128,0},{192,64},{1,129},{65,193},{129,1},{193,65... | collective-permute-start | bytes 3244040 | tf_op jit(solution)/shard_map/ppermute | solution.py:622
  72.1 1.4 copy-start.5
  89.4 2.8 %copy-start.1 = (f32[6,32,64,128]{3,2,1,0:T(8,128)S(1)}, f32[6,32,64,128]{3,2,1,0:T(8,128)}, u32[]{:S(2)}) copy-start(f32[6,32,64,128]{3,2,1,0:T(8,128)} %get-tuple-element.24.hpsi_ref) | copy-start | bytes 18874372
  98.4 5.1 %copy-start.8 = (bf16[6,7,64,128]{3,2,1,0:T(8,128)(2,1)S(1)}, bf16[6,7,64,128]{3,2,1,0:T(8,128)(2,1)}, u32[]{:S(2)}) copy-start(bf16[6,7,64,128]{3,2,1,0:T(8,128)(2,1)} %copy-done.7) | copy-start | bytes 2064388
  107.8 44.8 %copy-start = (bf16[64,6,32,128]{3,2,1,0:T(8,128)(2,1)S(1)}, bf16[64,6,32,128]{3,2,1,0:T(8,128)(2,1)}, u32[]{:S(2)}) copy-start(bf16[64,6,32,128]{3,2,1,0:T(8,128)(2,1)} %refs_1_.1) | copy-start | bytes 9437188
